TPU v7x, 32 devices: a whole 2x2x4 slice. The times are simulated.
32 devices in a mesh: dp: 4 (over z), fsdp: 8 (over y, x, core).
Axes of the slice: x: 2, y: 2, z: 4, core: 2. Of those that a mesh axis runs over, the one named last changes fastest.
Arguments:
- tokens: bfloat16 [4096, 1024], P(('dp', 'fsdp')), may hold values from -6 to 6
- seq_starts: int32 [4, 2], P('dp'), may hold values from 0 to 768, as said below
- expert_ids: int32 [4096, 8], P(('dp', 'fsdp')), may hold values from 0 to 31, all different within a row; in each aligned block of 128 rows (0 to 127, 128 to 255, ...) at most 48 rows name the same one
- attn_gain: bfloat16 [1024], P(('dp', 'fsdp')), may hold values from 0.099609375 to 1.8984375
- w_query: bfloat16 [1024, 1024], P(('dp', 'fsdp')), may hold values from -1 to 1
- key_weight: bfloat16 [1024, 512], P(('dp', 'fsdp')), may hold values from -1 to 1
- value_weight: bfloat16 [1024, 512], P(('dp', 'fsdp')), may hold values from -0.1875 to 0.1875
- w_output: bfloat16 [1024, 1024], P(('dp', 'fsdp')), may hold values from -3 to 3
- ffn_gain: bfloat16 [1024], P(('dp', 'fsdp')), may hold values from 0.099609375 to 1.8984375
- w_router: bfloat16 [1024, 32], P(('dp', 'fsdp')), may hold values from -1 to 1
- expert_in: bfloat16 [32, 1024, 1024], P('fsdp', 'dp'), may hold values from -0.1875 to 0.1875
- expert_out: bfloat16 [32, 512, 1024], P('fsdp', None, 'dp'), may hold values from -0.5 to 0.5
- d_out: bfloat16 [4096, 1024], P(('dp', 'fsdp')), may hold values from -6 to 6
Outputs:
- block_out: bfloat16 [4096, 1024], P(('dp', 'fsdp'))
- d_tokens: float32 [4096, 1024], P(('dp', 'fsdp'))
- d_attn_gain: float32 [1024], P(('dp', 'fsdp'))
- d_query: float32 [1024, 1024], P(('dp', 'fsdp'))
- d_key: float32 [1024, 512], P(('dp', 'fsdp'))
- d_value: float32 [1024, 512], P(('dp', 'fsdp'))
- d_output: float32 [1024, 1024], P(('dp', 'fsdp'))
- d_ffn_gain: float32 [1024], P(('dp', 'fsdp'))
- d_router: float32 [1024, 32], P(('dp', 'fsdp'))
- d_expert_in: float32 [32, 1024, 1024], P('fsdp', 'dp')
- d_expert_out: float32 [32, 512, 1024], P('fsdp', None, 'dp')
Inputs may be any that keep to these rules, and one draw needn't show every extreme that they name: seq_starts[g, 0] is 0 and seq_starts[g, 1] splits group g into two sequences of 256 tokens or more (group 0's second sequence has exactly 256). `expert_ids`: each row names 8 different experts; among the 128 rows of one device no expert is named more than 48 times.
All inputs are finite; a program needn't handle non-finite values.
Results may differ from a plain program's by a relative error of at most 0.015.
Values may be sent and summed in bfloat16 or wider, within the bound.
No kernel may reach another device: no remote copies, remote signals or barrier semaphores. Data moves between devices by JAX's collectives and lax.ppermute only.
A program may use at most 192 MiB of HBM per device.

v0:
```python
import math

import jax
import jax.numpy as jnp
from jax import lax
from jax.sharding import PartitionSpec as P

QUERY_HEADS = 16
KEY_HEADS = 8
HEAD_DIM = 64
CAP = 48


norm_eps = 1e-06
score_scale = 0.015625
rope_base = 10000.0
masked_low = -1e30


def norm_forward(values, gain_vec):
    scale_row = lax.rsqrt(jnp.mean(values * values, axis=-1, keepdims=True) + norm_eps)
    unit_row = values * scale_row
    return (unit_row, scale_row, (unit_row * gain_vec.astype(jnp.float32)).astype(jnp.bfloat16))


def norm_backward(d_normed, unit_row, scale_row, gain_vec):
    scaled = d_normed * gain_vec.astype(jnp.float32)
    grad_values = scale_row * (
        scaled - unit_row * jnp.mean(scaled * unit_row, axis=-1, keepdims=True)
    )
    return (grad_values, jnp.sum(d_normed * unit_row, axis=0))


def rope_tables(positions, head_size):
    half_index = jnp.arange(head_size // 2, dtype=jnp.float32)
    inverse = jnp.exp(half_index * (-2.0 * math.log(rope_base) / head_size))
    angles = positions.astype(jnp.float32)[:, None] * inverse[None, :]
    return (jnp.cos(angles), jnp.sin(angles))


def apply_rotation(values, cosine_table, sine_values):
    first_half, second_half = jnp.split(values, 2, axis=-1)
    cos_col = cosine_table[:, None, :]
    sin_col = sine_values[:, None, :]
    return jnp.concatenate(
        [
            first_half * cos_col - second_half * sin_col,
            second_half * cos_col + first_half * sin_col,
        ],
        axis=-1,
    )


def reverse_rotation(values, cosine_table, sine_values):
    first_half, second_half = jnp.split(values, 2, axis=-1)
    cos_col = cosine_table[:, None, :]
    sin_col = sine_values[:, None, :]
    return jnp.concatenate(
        [
            first_half * cos_col + second_half * sin_col,
            second_half * cos_col - first_half * sin_col,
        ],
        axis=-1,
    )


def key_width(tok_rows, fsdp_count):
    shards = 1
    while shards * 2 * tok_rows <= 1024 and fsdp_count % (shards * 2) == 0:
        shards = shards * 2
    return shards * tok_rows


def make_scores(grouped_rows, keys_all, query_positions, sequence_start, block_width):
    key_value_heads = grouped_rows.shape[1]
    head_size = grouped_rows.shape[3]

    def scores_at(block_no):
        begin_at = block_no * block_width
        key_blk = lax.dynamic_slice_in_dim(keys_all, begin_at, block_width, 0).reshape(
            block_width, key_value_heads, head_size
        )
        scores = (
            jnp.einsum("tgrd,kgd->tgrk", grouped_rows, key_blk, preferred_element_type=jnp.float32)
            * score_scale
        )
        key_pos = begin_at + jnp.arange(block_width, dtype=jnp.int32)
        allowed = (key_pos[None, :] <= query_positions[:, None]) & (
            key_pos[None, :] >= sequence_start[:, None]
        )
        return (key_blk, scores, allowed[:, None, None, :], begin_at)

    return scores_at


def attention_forward(scores_at, values_all, count_blocks, grouped_rows):
    lse_shape = grouped_rows.shape[:3]

    def first_pass(block_no, state_pair):
        row_max, summed = state_pair
        key_blk, scores, allowed, begin_at = scores_at(block_no)
        new_max = jnp.maximum(row_max, jnp.max(jnp.where(allowed, scores, masked_low), axis=-1))
        summed = summed * jnp.exp(row_max - new_max) + jnp.sum(
            jnp.where(allowed, jnp.exp(scores - new_max[..., None]), 0.0), axis=-1
        )
        return (new_max, summed)

    start_pair = (jnp.full(lse_shape, masked_low, jnp.float32), jnp.zeros(lse_shape, jnp.float32))
    row_max, summed = lax.fori_loop(0, count_blocks, first_pass, start_pair)
    log_sum_exponent = row_max + jnp.log(summed)

    def second_pass(block_no, result):
        key_blk, scores, allowed, begin_at = scores_at(block_no)
        val_blk = lax.dynamic_slice_in_dim(values_all, begin_at, key_blk.shape[0], 0).reshape(
            key_blk.shape
        )
        probs = jnp.where(allowed, jnp.exp(scores - log_sum_exponent[..., None]), 0.0).astype(
            jnp.bfloat16
        )
        return result + jnp.einsum(
            "tgrk,kgd->tgrd", probs, val_blk, preferred_element_type=jnp.float32
        )

    result = lax.fori_loop(0, count_blocks, second_pass, jnp.zeros(grouped_rows.shape, jnp.float32))
    return (result, log_sum_exponent)


def attention_backward(
    scores_at, values_all, count_blocks, grouped_rows, log_sum_exponent, grad_grouped, out_grouped
):
    output_dot_grad = jnp.sum(
        grad_grouped.astype(jnp.float32) * out_grouped.astype(jnp.float32), axis=-1
    )
    group_rows = values_all.shape[0]
    kv_width = values_all.shape[1]

    def one_step(block_no, state_all):
        d_queries, grad_keys, grad_values = state_all
        key_blk, scores, allowed, begin_at = scores_at(block_no)
        width_now = key_blk.shape[0]
        val_blk = lax.dynamic_slice_in_dim(values_all, begin_at, width_now, 0).reshape(
            key_blk.shape
        )
        probs = jnp.where(allowed, jnp.exp(scores - log_sum_exponent[..., None]), 0.0)
        d_val_blk = jnp.einsum(
            "tgrk,tgrd->kgd",
            probs.astype(jnp.bfloat16),
            grad_grouped,
            preferred_element_type=jnp.float32,
        )
        d_probs = jnp.einsum(
            "tgrd,kgd->tgrk", grad_grouped, val_blk, preferred_element_type=jnp.float32
        )
        d_scores = (probs * (d_probs - output_dot_grad[..., None]) * score_scale).astype(
            jnp.bfloat16
        )
        d_queries = d_queries + jnp.einsum(
            "tgrk,kgd->tgrd", d_scores, key_blk, preferred_element_type=jnp.float32
        )
        d_key_blk = jnp.einsum(
            "tgrk,tgrd->kgd", d_scores, grouped_rows, preferred_element_type=jnp.float32
        )
        grad_keys = lax.dynamic_update_slice_in_dim(
            grad_keys, d_key_blk.reshape(width_now, kv_width), begin_at, 0
        )
        grad_values = lax.dynamic_update_slice_in_dim(
            grad_values, d_val_blk.reshape(width_now, kv_width), begin_at, 0
        )
        return (d_queries, grad_keys, grad_values)

    start_all = (
        jnp.zeros(grouped_rows.shape, jnp.float32),
        jnp.zeros((group_rows, kv_width), jnp.float32),
        jnp.zeros((group_rows, kv_width), jnp.float32),
    )
    return lax.fori_loop(0, count_blocks, one_step, start_all)


def local(
    tokens,
    seq_starts,
    expert_ids,
    attn_gain,
    w_query,
    key_weight,
    value_weight,
    w_output,
    ffn_gain,
    w_router,
    expert_in,
    expert_out,
    d_out,
):
    fsdp_count = lax.axis_size("fsdp")
    tok_rows = tokens.shape[0]
    model_width = tokens.shape[1]
    local_experts = expert_in.shape[0]
    top_count = expert_ids.shape[1]
    experts_total = w_router.shape[1]
    capacity = CAP
    key_value_heads = KEY_HEADS
    head_size = HEAD_DIM
    query_heads = QUERY_HEADS
    heads_per_key = query_heads // key_value_heads
    gathered = (
        lax.all_gather(attn_gain, ("dp", "fsdp"), axis=0, tiled=True),
        lax.all_gather(w_query, ("dp", "fsdp"), axis=0, tiled=True),
        lax.all_gather(key_weight, ("dp", "fsdp"), axis=0, tiled=True),
        lax.all_gather(value_weight, ("dp", "fsdp"), axis=0, tiled=True),
        lax.all_gather(w_output, ("dp", "fsdp"), axis=0, tiled=True),
        lax.all_gather(ffn_gain, ("dp", "fsdp"), axis=0, tiled=True),
        lax.all_gather(w_router, ("dp", "fsdp"), axis=0, tiled=True),
    )
    gain_one, query_w, key_w, value_w, output_w, gain_two, router_w = gathered
    global_pos = lax.axis_index("fsdp") * tok_rows + jnp.arange(tok_rows, dtype=jnp.int32)
    second_start = seq_starts[0, 1]
    sequence_start = jnp.where(global_pos >= second_start, second_start, seq_starts[0, 0])
    cosine_table, sine_values = rope_tables(global_pos - sequence_start, head_size)
    tok_f32 = tokens.astype(jnp.float32)
    unit_one, scale_one, first_normed = norm_forward(tok_f32, gain_one)
    query_rows = apply_rotation(
        jnp.dot(first_normed, query_w, preferred_element_type=jnp.float32).reshape(
            tok_rows, query_heads, head_size
        ),
        cosine_table,
        sine_values,
    ).astype(jnp.bfloat16)
    key_matrix = apply_rotation(
        jnp.dot(first_normed, key_w, preferred_element_type=jnp.float32).reshape(
            tok_rows, key_value_heads, head_size
        ),
        cosine_table,
        sine_values,
    ).astype(jnp.bfloat16)
    value_matrix = jnp.dot(first_normed, value_w, preferred_element_type=jnp.float32).astype(
        jnp.bfloat16
    )
    key_flat = key_matrix.reshape(tok_rows, key_value_heads * head_size)
    keys_all, values_all = (
        lax.all_gather(key_flat, "fsdp", axis=0, tiled=True),
        lax.all_gather(value_matrix, "fsdp", axis=0, tiled=True),
    )
    grouped_rows = query_rows.reshape(tok_rows, key_value_heads, heads_per_key, head_size)
    block_width = key_width(tok_rows, fsdp_count)
    count_blocks = keys_all.shape[0] // block_width
    scores_at = make_scores(grouped_rows, keys_all, global_pos, sequence_start, block_width)
    attended_f32, log_sum_exponent = attention_forward(
        scores_at, values_all, count_blocks, grouped_rows
    )
    attended_rows = attended_f32.reshape(tok_rows, query_heads * head_size).astype(jnp.bfloat16)
    hidden = tok_f32 + jnp.dot(attended_rows, output_w, preferred_element_type=jnp.float32)
    unit_two, scale_two, normed_two = norm_forward(hidden, gain_two)
    logits = jnp.dot(normed_two, router_w, preferred_element_type=jnp.float32)
    gate_vals = jax.nn.softmax(jnp.take_along_axis(logits, expert_ids, axis=1), axis=-1)
    one_hot = (
        (expert_ids[:, :, None] == jnp.arange(experts_total, dtype=jnp.int32)[None, None, :])
        .astype(jnp.int32)
        .reshape(tok_rows * top_count, experts_total)
    )
    before = jnp.cumsum(one_hot, axis=0) - one_hot
    slot_pos = jnp.sum(before * one_hot, axis=1).reshape(tok_rows, top_count)
    dest_dev = expert_ids // local_experts
    local_exp = expert_ids % local_experts
    buffer_pos = ((local_exp * fsdp_count + dest_dev) * capacity + slot_pos).reshape(-1)
    buffer_rows = local_experts * fsdp_count * capacity
    send_buf = (
        jnp.zeros((buffer_rows, model_width), jnp.bfloat16)
        .at[buffer_pos]
        .set(jnp.repeat(normed_two, top_count, axis=0))
    )
    received = lax.all_to_all(
        send_buf.reshape(local_experts, fsdp_count * capacity, model_width),
        "fsdp",
        split_axis=1,
        concat_axis=1,
        tiled=True,
    )
    win_all, wout_all = (
        lax.all_gather(expert_in, "dp", axis=1, tiled=True),
        lax.all_gather(expert_out, "dp", axis=2, tiled=True),
    )
    gate_up = jnp.einsum("erd,edf->erf", received, win_all, preferred_element_type=jnp.float32)
    gate_part, up_part = jnp.split(gate_up, 2, axis=-1)
    activation = (jax.nn.silu(gate_part) * up_part).astype(jnp.bfloat16)
    expert_res = jnp.einsum(
        "erf,efd->erd", activation, wout_all, preferred_element_type=jnp.float32
    ).astype(jnp.bfloat16)
    returned = lax.all_to_all(expert_res, "fsdp", split_axis=1, concat_axis=1, tiled=True)
    chosen_out = returned.reshape(buffer_rows, model_width)[buffer_pos].reshape(
        tok_rows, top_count, model_width
    )
    mixture = jnp.sum(gate_vals[:, :, None] * chosen_out.astype(jnp.float32), axis=1)
    block_out = (hidden + mixture).astype(jnp.bfloat16)
    gathered_back = (
        lax.all_gather(attn_gain, ("dp", "fsdp"), axis=0, tiled=True),
        lax.all_gather(w_query, ("dp", "fsdp"), axis=0, tiled=True),
        lax.all_gather(key_weight, ("dp", "fsdp"), axis=0, tiled=True),
        lax.all_gather(value_weight, ("dp", "fsdp"), axis=0, tiled=True),
        lax.all_gather(w_output, ("dp", "fsdp"), axis=0, tiled=True),
        lax.all_gather(ffn_gain, ("dp", "fsdp"), axis=0, tiled=True),
        lax.all_gather(w_router, ("dp", "fsdp"), axis=0, tiled=True),
    )
    win_back, wout_back = (
        lax.all_gather(expert_in, "dp", axis=1, tiled=True),
        lax.all_gather(expert_out, "dp", axis=2, tiled=True),
    )
    gain_one_b, query_w_b, key_w_b, value_w_b, output_w_b, gain_two_b, router_w_b = gathered_back
    d_block = d_out.astype(jnp.float32)
    d_chosen = (gate_vals[:, :, None] * d_block[:, None, :]).astype(jnp.bfloat16)
    d_gate = jnp.sum(d_block[:, None, :] * chosen_out.astype(jnp.float32), axis=-1)
    d_send = (
        jnp.zeros((buffer_rows, model_width), jnp.bfloat16)
        .at[buffer_pos]
        .set(d_chosen.reshape(tok_rows * top_count, model_width))
    )
    d_received = lax.all_to_all(
        d_send.reshape(local_experts, fsdp_count * capacity, model_width),
        "fsdp",
        split_axis=1,
        concat_axis=1,
        tiled=True,
    )
    d_act = jnp.einsum("erd,efd->erf", d_received, wout_back, preferred_element_type=jnp.float32)
    sigmoid_g = jax.nn.sigmoid(gate_part)
    silu_g = gate_part * sigmoid_g
    d_gate_up = jnp.concatenate(
        [d_act * up_part * sigmoid_g * (1.0 + gate_part * (1.0 - sigmoid_g)), d_act * silu_g],
        axis=-1,
    ).astype(jnp.bfloat16)
    grad_out_local = jnp.einsum(
        "erf,erd->efd", activation, d_received, preferred_element_type=jnp.float32
    )
    grad_in_local = jnp.einsum(
        "erd,erf->edf", received, d_gate_up, preferred_element_type=jnp.float32
    )
    d_rows = jnp.einsum(
        "erf,edf->erd", d_gate_up, win_back, preferred_element_type=jnp.float32
    ).astype(jnp.bfloat16)
    d_returned = lax.all_to_all(d_rows, "fsdp", split_axis=1, concat_axis=1, tiled=True)
    d_from_experts = jnp.sum(
        d_returned.reshape(buffer_rows, model_width)[buffer_pos]
        .reshape(tok_rows, top_count, model_width)
        .astype(jnp.float32),
        axis=1,
    )
    d_expert_in, d_expert_out = (
        lax.psum_scatter(
            grad_in_local.astype(jnp.bfloat16), "dp", scatter_dimension=1, tiled=True
        ).astype(jnp.float32),
        lax.psum_scatter(
            grad_out_local.astype(jnp.bfloat16), "dp", scatter_dimension=2, tiled=True
        ).astype(jnp.float32),
    )
    d_sel = gate_vals * (d_gate - jnp.sum(gate_vals * d_gate, axis=-1, keepdims=True))
    d_logits = jnp.sum(
        one_hot.reshape(tok_rows, top_count, experts_total).astype(jnp.float32) * d_sel[:, :, None],
        axis=1,
    ).astype(jnp.bfloat16)
    grad_router = jnp.einsum("td,te->de", normed_two, d_logits, preferred_element_type=jnp.float32)
    d_normed_two = d_from_experts + jnp.einsum(
        "te,de->td", d_logits, router_w_b, preferred_element_type=jnp.float32
    )
    d_hidden_two, grad_gain_two = norm_backward(d_normed_two, unit_two, scale_two, gain_two_b)
    d_hidden = d_block + d_hidden_two
    d_hidden_b = d_hidden.astype(jnp.bfloat16)
    grad_output_w = jnp.einsum(
        "tc,td->cd", attended_rows, d_hidden_b, preferred_element_type=jnp.float32
    )
    grad_attended = jnp.einsum(
        "td,cd->tc", d_hidden_b, output_w_b, preferred_element_type=jnp.float32
    ).astype(jnp.bfloat16)
    grad_grouped = grad_attended.reshape(tok_rows, key_value_heads, heads_per_key, head_size)
    out_grouped = attended_rows.reshape(tok_rows, key_value_heads, heads_per_key, head_size)
    d_queries, d_keys_all, d_values_all = attention_backward(
        scores_at,
        values_all,
        count_blocks,
        grouped_rows,
        log_sum_exponent,
        grad_grouped,
        out_grouped,
    )
    d_keys_own, d_values_own = (
        lax.psum_scatter(
            d_keys_all.astype(jnp.bfloat16), "fsdp", scatter_dimension=0, tiled=True
        ).astype(jnp.float32),
        lax.psum_scatter(
            d_values_all.astype(jnp.bfloat16), "fsdp", scatter_dimension=0, tiled=True
        ).astype(jnp.float32),
    )
    d_query_b = (
        reverse_rotation(
            d_queries.reshape(tok_rows, query_heads, head_size), cosine_table, sine_values
        )
        .reshape(tok_rows, query_heads * head_size)
        .astype(jnp.bfloat16)
    )
    grad_key_block = (
        reverse_rotation(
            d_keys_own.reshape(tok_rows, key_value_heads, head_size), cosine_table, sine_values
        )
        .reshape(tok_rows, key_value_heads * head_size)
        .astype(jnp.bfloat16)
    )
    grad_value_block = d_values_own.astype(jnp.bfloat16)
    grad_query = jnp.einsum(
        "td,tc->dc", first_normed, d_query_b, preferred_element_type=jnp.float32
    )
    grad_key = jnp.einsum(
        "td,tc->dc", first_normed, grad_key_block, preferred_element_type=jnp.float32
    )
    grad_value = jnp.einsum(
        "td,tc->dc", first_normed, grad_value_block, preferred_element_type=jnp.float32
    )
    d_normed_one = jnp.einsum("tc,dc->td", d_query_b, query_w_b, preferred_element_type=jnp.float32)
    d_normed_one = d_normed_one + jnp.einsum(
        "tc,dc->td", grad_key_block, key_w_b, preferred_element_type=jnp.float32
    )
    d_normed_one = d_normed_one + jnp.einsum(
        "tc,dc->td", grad_value_block, value_w_b, preferred_element_type=jnp.float32
    )
    d_tok_one, grad_gain_one = norm_backward(d_normed_one, unit_one, scale_one, gain_one_b)
    d_tokens = d_hidden + d_tok_one
    summed_grads = (
        lax.psum_scatter(grad_gain_one, ("dp", "fsdp"), scatter_dimension=0, tiled=True),
        lax.psum_scatter(grad_query, ("dp", "fsdp"), scatter_dimension=0, tiled=True),
        lax.psum_scatter(grad_key, ("dp", "fsdp"), scatter_dimension=0, tiled=True),
        lax.psum_scatter(grad_value, ("dp", "fsdp"), scatter_dimension=0, tiled=True),
        lax.psum_scatter(grad_output_w, ("dp", "fsdp"), scatter_dimension=0, tiled=True),
        lax.psum_scatter(grad_gain_two, ("dp", "fsdp"), scatter_dimension=0, tiled=True),
        lax.psum_scatter(grad_router, ("dp", "fsdp"), scatter_dimension=0, tiled=True),
    )
    return (
        block_out,
        d_tokens,
        summed_grads[0],
        summed_grads[1],
        summed_grads[2],
        summed_grads[3],
        summed_grads[4],
        summed_grads[5],
        summed_grads[6],
        d_expert_in,
        d_expert_out,
    )


def solution(mesh):
    in_specs = (
        P(("dp", "fsdp"), None),
        P("dp", None),
        P(("dp", "fsdp"), None),
        P(("dp", "fsdp")),
        P(("dp", "fsdp"), None),
        P(("dp", "fsdp"), None),
        P(("dp", "fsdp"), None),
        P(("dp", "fsdp"), None),
        P(("dp", "fsdp")),
        P(("dp", "fsdp"), None),
        P("fsdp", "dp", None),
        P("fsdp", None, "dp"),
        P(("dp", "fsdp"), None),
    )
    out_specs = (
        P(("dp", "fsdp"), None),
        P(("dp", "fsdp"), None),
        P(("dp", "fsdp")),
        P(("dp", "fsdp"), None),
        P(("dp", "fsdp"), None),
        P(("dp", "fsdp"), None),
        P(("dp", "fsdp"), None),
        P(("dp", "fsdp")),
        P(("dp", "fsdp"), None),
        P("fsdp", "dp", None),
        P("fsdp", None, "dp"),
    )
    return jax.shard_map(local, mesh=mesh, in_specs=in_specs, out_specs=out_specs, check_vma=False)
```

profile of v0, /device:TPU:0, one launch (start us, length us, event | category | flops | bytes accessed | tf_op | source)
XLA Modules:
  0.0 1665.6 jit_solution(11584177746769389169)
XLA Ops:
  10.4 42.0 %all-reduce.5 = (bf16[1024]{0:T(1024)(128)(2,1)S(1)}, bf16[1024]{0:T(1024)(128)(2,1)S(1)}) all-reduce(bf16[1024]{0:T(1024)(128)(2,1)S(1)} %dynamic-update-slice, bf16[1024]{0:T(1024)(128)(2,1)S(1)} %dynamic-update-slice.1), channel_id=1, replica_groups=mesh['dp'=4,'fsdp'=8] {'dp','fsdp'}, use_global_device_ids=true, to_apply=%add | all-reduce | flops 2048 | bytes 8192
  53.5 13.7 all-gather.9.cloned.1.call-done
  73.0 49.7 %all-gather.13.cloned.1.call-done = bf16[1024,512]{1,0:T(8,128)(2,1)} async-done(((bf16[32,512]{1,0:T(8,128)(2,1)}), bf16[1024,512]{1,0:T(8,128)(2,1)}) %all-gather.13.cloned.1.call-update) | async-done | bytes 1048592 | tf_op jit(solution)/shard_map/all_gather | solution.py:208
  127.8 9.0 reduce-window.6
  138.4 9.2 all-gather.11.cloned.1.call-done
  149.2 57.4 %all-gather.17.cloned.1.call-done = bf16[1024,1024]{1,0:T(8,128)(2,1)} async-done(((bf16[32,1024]{1,0:T(8,128)(2,1)}), bf16[1024,1024]{1,0:T(8,128)(2,1)}) %all-gather.17.cloned.1.call-update) | async-done | bytes 2097168 | tf_op jit(solution)/shard_map/all_gather | solution.py:207
  209.3 22.0 %all-gather.15.cloned.1.call-done = bf16[1024,512]{0,1:T(8,128)(2,1)} async-done(((bf16[128,512]{0,1:T(8,128)(2,1)}), bf16[1024,512]{0,1:T(8,128)(2,1)}) %all-gather.15.cloned.1.call-update) | async-done | bytes 1048592 | tf_op jit(solution)/shard_map/all_gather | solution.py:240
  238.8 51.4 %all-gather.19.cloned.1.call-done = bf16[1024,1024]{1,0:T(8,128)(2,1)} async-done(((bf16[32,1024]{1,0:T(8,128)(2,1)}), bf16[1024,1024]{1,0:T(8,128)(2,1)}) %all-gather.19.cloned.1.call-update) | async-done | bytes 2097168 | tf_op jit(solution)/shard_map/all_gather | solution.py:210
  293.2 6.9 scatter_custom_fusion
  300.1 4.1 copy.203
  304.2 4.6 all-to-all-start
  309.9 70.7 %all_gather.50 = bf16[1024,32]{1,0:T(8,128)(2,1)S(1)} all-gather(bf16[32,32]{1,0:T(8,128)(2,1)S(1)} %copy-done.42), channel_id=1, replica_groups=mesh['dp'=4,'fsdp'=8] {'dp','fsdp'}, dimensions={0}, use_global_device_ids=true | all-gather | bytes 67584 | tf_op jit(solution)/shard_map/all_gather | solution.py:212
  381.6 7.0 gather_fusion.2
  390.7 7.4 scatter_custom_fusion.1
  398.2 4.1 copy.208
  402.2 4.8 all-to-all-start.2
  407.1 5.1 copy.218
  412.2 29.3 %all-gather.21.cloned.1.call-done = bf16[4,1024,1024]{2,1,0:T(8,128)(2,1)} async-done(((bf16[4,256,1024]{2,1,0:T(8,128)(2,1)}), bf16[4,1024,1024]{2,1,0:T(8,128)(2,1)}) %all-gather.21.cloned.1.call-update) | async-done | bytes 8388624 | tf_op jit(solution)/shard_map/all_gather | solution.py:279
  441.5 9.5 fusion.89
  451.0 70.9 %all-gather.23.cloned.1.call-done = bf16[4,512,1024]{2,1,0:T(8,128)(2,1)} async-done(((bf16[4,512,256]{2,1,0:T(8,128)(2,1)}), bf16[4,512,1024]{2,1,0:T(8,128)(2,1)}) %all-gather.23.cloned.1.call-update) | async-done | bytes 4194320 | tf_op jit(solution)/shard_map/all_gather | solution.py:280
  521.9 9.8 multiply_convert_fusion.1
  531.7 10.7 convolution_convert_fusion.1
  542.4 4.1 copy.210
  546.5 3.7 all-to-all-start.3
  550.2 4.5 convolution_convert_fusion.2
  554.7 4.1 copy.205
  558.8 29.3 %all-to-all-done.3 = bf16[4,384,1024]{2,0,1:T(4,128)(2,1)S(1)} async-done(((bf16[4,384,1024]{2,0,1:T(4,128)(2,1)}), bf16[4,384,1024]{2,0,1:T(4,128)(2,1)S(1)}, u32[]{:S(2)}, u32[]{:S(2)}) %all-to-all-start.3) | async-done | bytes 3145760 | tf_op jit(solution)/shard_map/all_to_all | solution.py:339
  589.7 4.5 all-to-all-start.1
  598.4 5.8 gather_fusion.1
  604.2 3.8 convert_reduce_fusion
  608.0 24.1 %all-to-all-done.1 = bf16[4,384,1024]{2,0,1:T(4,128)(2,1)} async-done(((bf16[4,384,1024]{2,0,1:T(4,128)(2,1)}), bf16[4,384,1024]{2,0,1:T(4,128)(2,1)}, u32[]{:S(2)}, u32[]{:S(2)}) %all-to-all-start.1) | async-done | bytes 3145760 | tf_op jit(solution)/shard_map/all_to_all | solution.py:288
  634.9 5.6 gather_fusion
  640.6 4.4 fusion.11
  651.4 6.1 fusion.2
  662.3 5.0 bitcast_convert_fusion
  669.1 6.8 fusion.18
  677.3 10.1 convolution_convert_fusion
  689.6 6.6 reduce-scatter.28.cloned.1.call-done
  699.4 35.8 %reduce-scatter.30.cloned.1.call-done = bf16[128,512]{1,0:T(8,128)(2,1)} async-done(((bf16[1024,512]{1,0:T(8,128)(2,1)}), bf16[128,512]{1,0:T(8,128)(2,1)}) %reduce-scatter.30.cloned.1.call-update) | async-done | bytes 131088
  751.7 43.6 %all-reduce.4 = (f32[1024]{0:T(1024)S(1)}, f32[1024]{0:T(1024)S(1)}) all-reduce(f32[1024]{0:T(1024)S(1)} %get-tuple-element.79, f32[1024]{0:T(1024)S(1)} %copy-done.41), channel_id=4, replica_groups=mesh['dp'=4,'fsdp'=8] {'dp','fsdp'}, use_global_device_ids=true, to_apply=%region_22.23.clone | all-reduce | flops 2048 | bytes 16384
  797.5 17.9 %reduce-scatter.26.cloned.1.call-done = bf16[4,512,256]{2,1,0:T(8,128)(2,1)} async-done(((bf16[4,512,1024]{2,1,0:T(8,128)(2,1)}), bf16[4,512,256]{2,1,0:T(8,128)(2,1)}) %reduce-scatter.26.cloned.1.call-update) | async-done | bytes 1048592 | tf_op jit(solution)/shard_map/reduce_scatter | solution.py:350
  818.1 144.6 %reduce-scatter.24.cloned.1.call-done = bf16[4,256,1024]{2,1,0:T(8,128)(2,1)} async-done(((bf16[4,1024,1024]{2,1,0:T(8,128)(2,1)}), bf16[4,256,1024]{2,1,0:T(8,128)(2,1)}) %reduce-scatter.24.cloned.1.call-update) | async-done | bytes 2097168 | tf_op jit(solution)/shard_map/reduce_scatter | solution.py:347
  962.7 4.1 convert_element_type.203
  966.8 135.1 %reduce-scatter.22.cloned.1.call-done = f32[32,32]{1,0:T(8,128)} async-done(((f32[1024,32]{1,0:T(8,128)}), f32[32,32]{1,0:T(8,128)}) %reduce-scatter.22.cloned.1.call-update) | async-done | bytes 4112 | tf_op jit(solution)/shard_map/reduce_scatter | solution.py:431
  1101.9 137.1 %reduce-scatter.16.cloned.1.call-done = f32[32,512]{1,0:T(8,128)} async-done(((f32[1024,512]{1,0:T(8,128)}), f32[32,512]{1,0:T(8,128)}) %reduce-scatter.16.cloned.1.call-update) | async-done | bytes 65552 | tf_op jit(solution)/shard_map/reduce_scatter | solution.py:427
  1239.0 137.0 %reduce-scatter.18.cloned.1.call-done = f32[32,512]{1,0:T(8,128)} async-done(((f32[1024,512]{1,0:T(8,128)}), f32[32,512]{1,0:T(8,128)}) %reduce-scatter.18.cloned.1.call-update) | async-done | bytes 65552 | tf_op jit(solution)/shard_map/reduce_scatter | solution.py:428
  1375.9 141.7 %reduce-scatter.14.cloned.1.call-done = f32[32,1024]{1,0:T(8,128)} async-done(((f32[1024,1024]{1,0:T(8,128)}), f32[32,1024]{1,0:T(8,128)}) %reduce-scatter.14.cloned.1.call-update) | async-done | bytes 131088 | tf_op jit(solution)/shard_map/reduce_scatter | solution.py:426
  1517.7 141.2 %reduce-scatter.20.cloned.1.call-done = f32[32,1024]{1,0:T(8,128)} async-done(((f32[1024,1024]{1,0:T(8,128)}), f32[32,1024]{1,0:T(8,128)}) %reduce-scatter.20.cloned.1.call-update) | async-done | bytes 131088 | tf_op jit(solution)/shard_map/reduce_scatter | solution.py:429
  (236 shorter events, 84.7 us)
Async XLA Ops:
  7.2 60.0 %all-gather.9.cloned.1.call-start = ((), (), s32[]{:S(2)}) async-start(), calls=%async_computation.13 | async-start | bytes 1081344 | tf_op jit(solution)/shard_map/all_gather | solution.py:209
  7.9 114.8 %all-gather.13.cloned.1.call-start = ((), (), s32[]{:S(2)}) async-start(), calls=%async_computation.15 | async-start | bytes 1081344 | tf_op jit(solution)/shard_map/all_gather | solution.py:208
  8.7 139.0 %all-gather.11.cloned.1.call-start = ((), (), s32[]{:S(2)}) async-start(), calls=%async_computation.14 | async-start | bytes 1179648 | tf_op jit(solution)/shard_map/all_gather | solution.py:241
  52.4 154.2 %copy-start.28 = (f32[1024]{0:T(1024)}, f32[1024]{0:T(1024)S(1)}, u32[]{:S(2)}) copy-start(f32[1024]{0:T(1024)S(1)} %convert_element_type.163) | copy-start | bytes 12292
  53.5 153.1 %copy-start.39 = (f32[128]{0:T(128)}, f32[128]{0:T(128)S(1)}, u32[]{:S(2)}) copy-start(f32[128]{0:T(128)S(1)} %add_rsqrt_fusion.1) | copy-start | bytes 1540
  69.5 57.9 %copy-start.30 = (s32[128,8]{0,1:T(8,128)S(1)}, s32[128,8]{0,1:T(8,128)}, u32[]{:S(2)}) copy-start(s32[128,8]{0,1:T(8,128)} %param.15) | copy-start | bytes 12292
  69.6 137.0 %all-gather.17.cloned.1.call-start = ((), (), s32[]{:S(2)}) async-start(), calls=%async_computation.17 | async-start | bytes 2162688 | tf_op jit(solution)/shard_map/all_gather | solution.py:207
  70.2 161.1 %all-gather.15.cloned.1.call-start = ((), (), s32[]{:S(2)}) async-start(), calls=%async_computation.16 | async-start | bytes 1179648 | tf_op jit(solution)/shard_map/all_gather | solution.py:240
  73.0 136.2 %copy-start.26 = (f32[128,32]{0,1:T(8,128)}, f32[128,32]{0,1:T(8,128)S(1)}, u32[]{:S(2)}) copy-start(f32[128,32]{0,1:T(8,128)S(1)} %get-tuple-element.127) | copy-start | bytes 49156
  125.4 164.8 %all-gather.19.cloned.1.call-start = ((), (), s32[]{:S(2)}) async-start(), calls=%async_computation.18 | async-start | bytes 2162688 | tf_op jit(solution)/shard_map/all_gather | solution.py:210
  125.9 80.7 %copy-start.2 = (bf16[128,1024]{1,0:T(8,128)(2,1)S(1)}, bf16[128,1024]{1,0:T(8,128)(2,1)}, u32[]{:S(2)}) copy-start(bf16[128,1024]{1,0:T(8,128)(2,1)} %param.13) | copy-start | bytes 786436
  126.0 315.5 %all-gather.21.cloned.1.call-start = ((), (), s32[]{:S(2)}) async-start(), calls=%async_computation.19 | async-start | bytes 10485760 | tf_op jit(solution)/shard_map/all_gather | solution.py:279
  126.7 395.2 %all-gather.23.cloned.1.call-start = ((), (), s32[]{:S(2)}) async-start(), calls=%async_computation.20 | async-start | bytes 5242880 | tf_op jit(solution)/shard_map/all_gather | solution.py:280
  127.8 164.6 %copy-start.35 = (f32[1024]{0:T(1024)}, f32[1024]{0:T(1024)S(1)}, u32[]{:S(2)}) copy-start(f32[1024]{0:T(1024)S(1)} %convert_element_type.172) | copy-start | bytes 12292
  149.1 86.6 %copy-start.23 = (bf16[1024,512]{0,1:T(8,128)(2,1)}, bf16[1024,512]{0,1:T(8,128)(2,1)S(1)}, u32[]{:S(2)}) copy-start(bf16[1024,512]{0,1:T(8,128)(2,1)S(1)} %copy.186) | copy-start | bytes 3145732
  209.3 24.7 %copy-start.18 = (bf16[128,16,32]{0,2,1:T(8,128)(2,1)}, bf16[128,16,32]{0,2,1:T(8,128)(2,1)S(1)}, u32[]{:S(2)}) copy-start(bf16[128,16,32]{0,2,1:T(8,128)(2,1)S(1)} %get-tuple-element.105) | copy-start | bytes 393220
  209.3 24.7 %copy-start.20 = (bf16[128,16,32]{0,2,1:T(8,128)(2,1)}, bf16[128,16,32]{0,2,1:T(8,128)(2,1)S(1)}, u32[]{:S(2)}) copy-start(bf16[128,16,32]{0,2,1:T(8,128)(2,1)S(1)} %get-tuple-element.106) | copy-start | bytes 393220
  238.8 54.4 %copy-start.16 = (bf16[8,64,128,2]{2,1,3,0:T(8,128)(2,1)}, bf16[8,64,128,2]{2,1,3,0:T(8,128)(2,1)S(1)}, u32[]{:S(2)}) copy-start(bf16[8,64,128,2]{2,1,3,0:T(8,128)(2,1)S(1)} %convolution_convert_fusion.4) | copy-start | bytes 786436
  304.2 4.6 copy-start.22
  304.2 5.5 copy-start.31
  304.2 5.7 copy-start.42
  304.2 77.1 %copy-start.9 = (bf16[128,1024]{1,0:T(8,128)(2,1)S(1)}, bf16[128,1024]{1,0:T(8,128)(2,1)}, u32[]{:S(2)}) copy-start(bf16[128,1024]{1,0:T(8,128)(2,1)} %multiply_convert_fusion.3) | copy-start | bytes 786436
  304.2 98.0 %all-to-all-start = ((bf16[4,384,1024]{2,0,1:T(4,128)(2,1)}), bf16[4,384,1024]{2,0,1:T(4,128)(2,1)}, u32[]{:S(2)}, u32[]{:S(2)}) async-start(bf16[4,384,1024]{2,0,1:T(4,128)(2,1)} %copy.203), calls=%async_computation | async-start | bytes 6291456 | tf_op jit(solution)/shard_map/all_to_all | solution.py:271
  402.2 119.6 %all-to-all-start.2 = ((bf16[4,384,1024]{2,0,1:T(4,128)(2,1)}), bf16[4,384,1024]{2,0,1:T(4,128)(2,1)}, u32[]{:S(2)}, u32[]{:S(2)}) async-start(bf16[4,384,1024]{2,0,1:T(4,128)(2,1)} %copy.208), calls=%async_computation.2 | async-start | bytes 6291456 | tf_op jit(solution)/shard_map/all_to_all | solution.py:316
  412.2 38.7 %copy-start.13 = (bf16[4,384,1024]{1,2,0:T(8,128)(2,1)}, bf16[4,384,1024]{1,2,0:T(8,128)(2,1)S(1)}, u32[]{:S(2)}) copy-start(bf16[4,384,1024]{1,2,0:T(8,128)(2,1)S(1)} %copy.218) | copy-start | bytes 9437188
  531.7 10.7 copy-start.49
  531.7 10.7 copy-start.51
  546.5 41.5 %all-to-all-start.3 = ((bf16[4,384,1024]{2,0,1:T(4,128)(2,1)}), bf16[4,384,1024]{2,0,1:T(4,128)(2,1)S(1)}, u32[]{:S(2)}, u32[]{:S(2)}) async-start(bf16[4,384,1024]{2,0,1:T(4,128)(2,1)} %copy.210), calls=%async_computation.3 | async-start | bytes 6291456 | tf_op jit(solution)/shard_map/all_to_all | solution.py:339
  589.7 42.4 %all-to-all-start.1 = ((bf16[4,384,1024]{2,0,1:T(4,128)(2,1)}), bf16[4,384,1024]{2,0,1:T(4,128)(2,1)}, u32[]{:S(2)}, u32[]{:S(2)}) async-start(bf16[4,384,1024]{2,0,1:T(4,128)(2,1)} %copy.205), calls=%async_computation.1 | async-start | bytes 6291456 | tf_op jit(solution)/shard_map/all_to_all | solution.py:288
  594.2 102.0 %reduce-scatter.28.cloned.1.call-start = ((), (), s32[]{:S(2)}) async-start(), calls=%async_computation.28 | async-start | bytes 1179648
  640.5 4.6 copy-start.15
  640.5 4.6 copy-start.36
  640.5 4.6 copy-start.47
  640.6 8.7 copy-start.7
  651.4 8.1 copy-start.19
  651.4 8.1 copy-start.21
  662.2 73.0 %reduce-scatter.30.cloned.1.call-start = ((), (), s32[]{:S(2)}) async-start(), calls=%async_computation.29 | async-start | bytes 1179648
  668.7 146.7 %reduce-scatter.26.cloned.1.call-start = ((), (), s32[]{:S(2)}) async-start(), calls=%async_computation.27 | async-start | bytes 5242880 | tf_op jit(solution)/shard_map/reduce_scatter | solution.py:350
  676.0 286.7 %reduce-scatter.24.cloned.1.call-start = ((), (), s32[]{:S(2)}) async-start(), calls=%async_computation.26 | async-start | bytes 10485760 | tf_op jit(solution)/shard_map/reduce_scatter | solution.py:347
  687.5 9.8 copy-start.27
  687.5 9.9 copy-start.29
  687.5 9.9 copy-start.40
  687.5 414.3 %reduce-scatter.22.cloned.1.call-start = ((), (), s32[]{:S(2)}) async-start(), calls=%async_computation.25 | async-start | bytes 540672 | tf_op jit(solution)/shard_map/reduce_scatter | solution.py:431
  689.5 549.5 %reduce-scatter.16.cloned.1.call-start = ((), (), s32[]{:S(2)}) async-start(), calls=%async_computation.22 | async-start | bytes 2162688 | tf_op jit(solution)/shard_map/reduce_scatter | solution.py:427
  699.3 38.8 %copy-start.8 = (bf16[1024,512]{0,1:T(8,128)(2,1)S(1)}, bf16[1024,512]{0,1:T(8,128)(2,1)}, u32[]{:S(2)}) copy-start(bf16[1024,512]{0,1:T(8,128)(2,1)} %all-gather.15.cloned.1.call-done) | copy-start | bytes 3145732
  699.3 676.6 %reduce-scatter.18.cloned.1.call-start = ((), (), s32[]{:S(2)}) async-start(), calls=%async_computation.23 | async-start | bytes 2162688 | tf_op jit(solution)/shard_map/reduce_scatter | solution.py:428
  738.0 779.6 %reduce-scatter.14.cloned.1.call-start = ((), (), s32[]{:S(2)}) async-start(), calls=%async_computation.21 | async-start | bytes 4325376 | tf_op jit(solution)/shard_map/reduce_scatter | solution.py:426
  744.2 914.6 %reduce-scatter.20.cloned.1.call-start = ((), (), s32[]{:S(2)}) async-start(), calls=%async_computation.24 | async-start | bytes 4325376 | tf_op jit(solution)/shard_map/reduce_scatter | solution.py:429
  (25 other events, 50.6 us)
Sparse Core Ops, SparseCore 0:
  10.8 56.3 all-gather.8
  70.1 52.5 all-gather.12
  125.2 22.4 all-gather.10
  150.4 56.1 all-gather.16
  208.9 22.3 all-gather.14
  234.0 56.1 all-gather.18
  291.8 149.6 all-gather.20
  443.0 78.8 all-gather.22
  662.3 33.8 reduce-scatter.27
  699.2 35.9 reduce-scatter.29
  737.5 77.8 reduce-scatter.25
  817.6 145.0 reduce-scatter.23
  965.5 136.3 reduce-scatter.21
  1104.6 134.3 reduce-scatter.15
  1241.7 134.2 reduce-scatter.17
  1378.6 138.9 reduce-scatter.13
  1520.4 138.4 reduce-scatter.19
where the time goes:
time: 1670 us
  waiting for transfers between devices  1260 us (75%)
  blocking collectives  156 us (9%)
  matrix products  96.4 us (6%)
  local copies, waits for them, and re-layouts  76.4 us (5%)
  other arithmetic  44.9 us (3%)
  starting transfers between devices  18.7 us (1%)
    reduce_scatter x1, waiting for transfers between devices, local(): lax.psum_scatter(grad_in_local.astype(jnp.bfloat16), 'dp', scatter_dimens...  145 us
    reduce_scatter x1, waiting for transfers between devices, local(): lax.psum_scatter(grad_query, ('dp', 'fsdp'), scatter_dimension=0, tiled=T...  142 us
    reduce_scatter x1, waiting for transfers between devices, local(): lax.psum_scatter(grad_output_w, ('dp', 'fsdp'), scatter_dimension=0, tile...  141 us
    reduce_scatter x1, waiting for transfers between devices, local(): lax.psum_scatter(grad_key, ('dp', 'fsdp'), scatter_dimension=0, tiled=True)  137 us
    reduce_scatter x1, waiting for transfers between devices, local(): lax.psum_scatter(grad_value, ('dp', 'fsdp'), scatter_dimension=0, tiled=T...  137 us
    reduce_scatter x1, waiting for transfers between devices, local(): lax.psum_scatter(grad_router, ('dp', 'fsdp'), scatter_dimension=0, tiled=...  135 us
    unnamed x2, blocking collectives  85.6 us
    all_gather x1, waiting for transfers between devices, local(): lax.all_gather(expert_out, 'dp', axis=2, tiled=True)  70.9 us
  transfers between devices with their start and end apart: 21, of which 19 were waited for; matrix products, arithmetic and copies ran while one was open for 9% of the time, Pallas kernels for 0%

commit v1 on v0

v1 whole, which is shorter than its diff:
```python
import math

import jax
import jax.numpy as jnp
from jax import lax
from jax.experimental import pallas as pl
from jax.experimental.pallas import tpu as pltpu
from jax.sharding import PartitionSpec as P


QUERY_HEADS = 16
KEY_HEADS = 8
HEAD_DIM = 64
CAP = 48
POOL_PLANES = 2
POOL_SHARDS = 16
PAD = 128


norm_eps = 1e-06
score_scale = 0.015625
rope_base = 10000.0
masked_low = -1e30

f32 = jnp.float32
bf16 = jnp.bfloat16


def swap(values, axis, mask):
    count = lax.axis_size(axis)
    return lax.ppermute(values, axis, [(i, i ^ mask) for i in range(count)])


def dot(left, right, dims):
    return lax.dot_general(left, right, (dims, ((), ())), preferred_element_type=f32)


def norm_backward(d_normed, unit_row, scale_row, gain_row):
    scaled = d_normed * gain_row
    grad_values = scale_row * (
        scaled - unit_row * jnp.mean(scaled * unit_row, axis=-1, keepdims=True)
    )
    return (grad_values, jnp.sum(d_normed * unit_row, axis=0))


def rope_tables(positions, head_size):
    half_index = jnp.arange(head_size // 2, dtype=f32)
    inverse = jnp.exp(half_index * (-2.0 * math.log(rope_base) / head_size))
    angles = positions.astype(f32)[:, None] * inverse[None, :]
    return (jnp.cos(angles), jnp.sin(angles))


def apply_rotation(values, cosine_table, sine_values):
    first_half, second_half = jnp.split(values, 2, axis=-1)
    cos_col = cosine_table[:, None, :]
    sin_col = sine_values[:, None, :]
    return jnp.concatenate(
        [
            first_half * cos_col - second_half * sin_col,
            second_half * cos_col + first_half * sin_col,
        ],
        axis=-1,
    )


def ordered(pieces, index):
    if len(pieces) == 1:
        return pieces
    half = len(pieces) // 2
    low, high = ordered(pieces[:half], index), ordered(pieces[half:], index)
    flip = (index & half) != 0
    return [jnp.where(flip, y, x) for x, y in zip(low, high)] + [
        jnp.where(flip, x, y) for x, y in zip(low, high)
    ]


def chip_masks():
    return [2 * c for c in range(1, lax.axis_size("fsdp") // 2)]


def gather_planes(rows, count):
    if count == 1:
        return rows
    pieces = [rows] + [swap(rows, "dp", k) for k in range(1, count)]
    return jnp.concatenate(pieces, axis=0)


def gather_pieces(rows, planes):
    first = gather_planes(rows, planes)
    half = [first] + [swap(first, "fsdp", m) for m in chip_masks()]
    return half + [swap(piece, "fsdp", 1) for piece in half]


def after(values, event):
    return values if event is None else lax.optimization_barrier((values, event))[0]


def scatter_chips(own_half, other_half, lead, event=None):
    total = own_half.astype(f32) + swap(other_half.astype(bf16), "fsdp", 1).astype(f32)
    parts = total.astype(bf16)
    out = total[:lead]
    for c, m in enumerate(chip_masks(), 1):
        piece = swap(parts[c * lead : (c + 1) * lead], "fsdp", m)
        piece = after(piece, event)
        out = out + piece.astype(f32)
    return out


def scatter_all(own_half, other_half, rows, count, events=(None, None)):
    planes = scatter_chips(own_half, other_half, count * rows, events[0])
    parts = planes.astype(bf16)
    out = planes[:rows]
    for k in range(1, count):
        piece = swap(parts[k * rows : (k + 1) * rows], "dp", k)
        out = out + after(piece, events[1]).astype(f32)
    return out


def gather_rows(rows, planes):
    first = gather_planes(rows, planes)
    half = jnp.concatenate([first] + [swap(first, "fsdp", m) for m in chip_masks()], axis=0)
    return [half, swap(half, "fsdp", 1)]


def expert_kernel(pieces, planes, held, tok_rows, width, ff, experts_total):
    blocks = pieces * planes
    half = pieces // 2
    contract_last = ((1,), (1,))
    contract_first = ((0,), (0,))

    def mm(left, right, dims=((1,), (0,))):
        return lax.dot_general(left, right, (dims, ((), ())), preferred_element_type=f32)

    def kernel(*refs):
        first_ref, router_ref, chosen_ref, slot_ref, win_ref, wout_ref = refs[:6]
        tok_refs = refs[6 : 6 + pieces]
        cot_refs = refs[6 + pieces : 6 + 2 * pieces]
        outs = refs[6 + 2 * pieces :]
        back_refs, mix_refs = outs[0:2], outs[2:4]
        gin_ref, gout_ref, rows_ref, drows_ref, gate_ref, back_rows_ref, mix_rows_ref = outs[4:]
        first = first_ref[0]
        slot_axis = lax.broadcasted_iota(jnp.int32, (CAP, tok_rows), 0)
        expert_axis = lax.broadcasted_iota(jnp.int32, (experts_total, planes * tok_rows), 0)

        def selection(block):
            return [slot_axis == slot_ref[block, e : e + 1, :] for e in range(held)]

        def stacked(parts):
            parts = [x.astype(f32) for x in parts]
            out = parts[0] if held == 1 else jnp.concatenate(parts, axis=0)
            return out.astype(bf16)

        for i in range(pieces):
            logits = mm(router_ref[...], tok_refs[i][...], contract_last)
            chosen = chosen_ref[i] > 0.0
            top = jnp.max(jnp.where(chosen, logits, masked_low), axis=0, keepdims=True)
            raised = jnp.where(chosen, jnp.exp(logits - top), 0.0)
            gates = raised / jnp.sum(raised, axis=0, keepdims=True)
            mine = [
                jnp.sum(jnp.where(expert_axis == first + e, gates, 0.0), axis=0, keepdims=True)
                for e in range(held)
            ]
            for a in range(planes):
                block = i * planes + a
                at = slice(a * tok_rows, (a + 1) * tok_rows)
                picks = selection(block)
                for e in range(held):
                    gate_ref[e, block * CAP : (block + 1) * CAP, :] = jnp.sum(
                        jnp.where(picks[e], mine[e][:, at], 0.0), axis=1, keepdims=True
                    )
                pick = stacked(picks)
                rows_ref[block] = mm(pick, tok_refs[i][at, :]).astype(bf16)
                drows_ref[block] = mm(pick, cot_refs[i][at, :width]).astype(bf16)

        lane = lax.broadcasted_iota(jnp.int32, (blocks * CAP, PAD), 1)
        for e in range(held):
            strip = slice(e * CAP, (e + 1) * CAP)
            rows = rows_ref[:, strip, :].reshape(blocks * CAP, width)
            gate = gate_ref[e]
            gate_up = mm(rows, win_ref[e])
            gate_part, up_part = gate_up[:, :ff], gate_up[:, ff:]
            sigmoid_g = 1.0 / (1.0 + jnp.exp(-gate_part))
            silu_g = gate_part * sigmoid_g
            activation = (silu_g * up_part).astype(bf16)
            result = mm(activation, wout_ref[e]).astype(bf16).astype(f32)
            mix_rows_ref[:, strip, :] = (gate * result).astype(bf16).reshape(blocks, CAP, width)
            d_rows = drows_ref[:, strip, :].reshape(blocks * CAP, width).astype(f32)
            d_gate = jnp.sum(d_rows * result, axis=1, keepdims=True)
            high = d_gate.astype(bf16).astype(f32)
            cols = jnp.where(
                lane == first + e,
                high,
                jnp.where(lane == first + e + experts_total, d_gate - high, 0.0),
            )
            back_rows_ref[:, strip, width:] = cols.astype(bf16).reshape(blocks, CAP, PAD)
            d_result = (gate * d_rows).astype(bf16)
            gout_ref[e] = mm(activation, d_result, contract_first).astype(bf16)
            d_act = mm(d_result, wout_ref[e], contract_last)
            d_gate_up = jnp.concatenate(
                [
                    d_act * up_part * sigmoid_g * (1.0 + gate_part * (1.0 - sigmoid_g)),
                    d_act * silu_g,
                ],
                axis=1,
            ).astype(bf16)
            back_rows_ref[:, strip, :width] = (
                mm(d_gate_up, win_ref[e], contract_last).astype(bf16).reshape(blocks, CAP, width)
            )
            gin_ref[e] = mm(rows, d_gate_up, contract_first).astype(bf16)

        for block in range(blocks):
            pick = stacked(selection(block))
            side, place = divmod(block, half * planes)
            at = slice(place * tok_rows, (place + 1) * tok_rows)
            back_refs[side][at, :] = mm(pick, back_rows_ref[block], contract_first).astype(bf16)
            mix_refs[side][at, :] = mm(pick, mix_rows_ref[block], contract_first).astype(bf16)

    side_rows = half * planes * tok_rows
    in_vmem = pl.BlockSpec(memory_space=pltpu.VMEM)
    return pl.pallas_call(
        kernel,
        out_shape=[jax.ShapeDtypeStruct((side_rows, width + PAD), bf16)] * 2
        + [jax.ShapeDtypeStruct((side_rows, width), bf16)] * 2
        + [
            jax.ShapeDtypeStruct((held, width, 2 * ff), bf16),
            jax.ShapeDtypeStruct((held, ff, width), bf16),
        ],
        in_specs=[pl.BlockSpec(memory_space=pltpu.SMEM)] + [in_vmem] * (5 + 2 * pieces),
        out_specs=[in_vmem] * 6,
        scratch_shapes=[
            pltpu.VMEM((blocks, held * CAP, width), bf16),
            pltpu.VMEM((blocks, held * CAP, width), bf16),
            pltpu.VMEM((held, blocks * CAP, 1), f32),
            pltpu.VMEM((blocks, held * CAP, width + PAD), bf16),
            pltpu.VMEM((blocks, held * CAP, width), bf16),
        ],
        compiler_params=pltpu.CompilerParams(vmem_limit_bytes=60 * 1024 * 1024),
        name="experts",
    )


def local(
    tokens,
    seq_starts,
    expert_ids,
    attn_gain,
    w_query,
    key_weight,
    value_weight,
    w_output,
    ffn_gain,
    w_router,
    expert_in,
    expert_out,
    d_out,
):
    fsdp_count = lax.axis_size("fsdp")
    dp_count = lax.axis_size("dp")
    fsdp_at = lax.axis_index("fsdp")
    dp_at = lax.axis_index("dp")
    chips = fsdp_count // 2
    tok_rows, width = tokens.shape
    own_rows = w_query.shape[0]
    local_experts, slice_width, ff_two = expert_in.shape
    ff = ff_two // 2
    experts_total = w_router.shape[1]
    planes = POOL_PLANES
    if local_experts % planes or dp_count % planes or planes * fsdp_count > POOL_SHARDS:
        planes = 1
    held = local_experts // planes
    heads_per_key = QUERY_HEADS // KEY_HEADS
    q_width = QUERY_HEADS * HEAD_DIM
    kv_width = KEY_HEADS * HEAD_DIM

    pack_one = jnp.concatenate(
        [w_query, key_weight, value_weight, attn_gain[:, None], jnp.zeros((own_rows, PAD - 1), bf16)],
        axis=1,
    )
    pack_two = jnp.concatenate(
        [
            w_output,
            w_router,
            ffn_gain[:, None],
            jnp.zeros((own_rows, PAD - experts_total - 1), bf16),
        ],
        axis=1,
    )
    qkv_pieces = gather_pieces(pack_one, dp_count)
    output_own, output_other = gather_rows(pack_two, dp_count)

    rel = jnp.arange(width, dtype=jnp.int32)
    rel_row = rel % own_rows
    rel_dp = (rel // own_rows) % dp_count
    rel_chip = (rel // (own_rows * dp_count)) % chips
    rel_core = rel // (own_rows * dp_count * chips)
    place = (
        (rel_dp ^ dp_at) * fsdp_count + ((2 * rel_chip + rel_core) ^ fsdp_at)
    ) * own_rows + rel_row
    shuffle = (place[None, :] == jnp.arange(width, dtype=jnp.int32)[:, None]).astype(bf16)
    half_width = width // 2

    small_own, small_other = output_own[:, width:], output_other[:, width:]
    small_all = (
        dot(shuffle[:, :half_width], small_own, ((1,), (0,)))
        + dot(shuffle[:, half_width:], small_other, ((1,), (0,)))
    ).astype(bf16)
    router_w = small_all[:, :experts_total]
    gain_two = small_all[:, experts_total].astype(f32)[None, :]

    d_pack = jnp.concatenate(
        [d_out, expert_ids.astype(bf16), jnp.zeros((tok_rows, PAD - expert_ids.shape[1]), bf16)],
        axis=1,
    )
    d_pool = gather_pieces(d_pack, planes)

    group_at = dp_at % planes
    in_groups = expert_in.reshape(planes, held, slice_width, ff_two)
    out_groups = expert_out.reshape(planes, held, ff, slice_width)
    in_parts, out_parts = [], []
    for k in range(dp_count):
        target = group_at ^ (k % planes)
        in_piece = lax.dynamic_index_in_dim(in_groups, target, 0, keepdims=False)
        out_piece = lax.dynamic_index_in_dim(out_groups, target, 0, keepdims=False)
        in_parts.append(in_piece if k == 0 else swap(in_piece, "dp", k))
        out_parts.append(out_piece if k == 0 else swap(out_piece, "dp", k))
    token_index = jnp.arange(tok_rows, dtype=jnp.int32)
    global_pos = fsdp_at * tok_rows + token_index
    second_start = seq_starts[0, 1]
    sequence_start = jnp.where(global_pos >= second_start, second_start, seq_starts[0, 0])
    cosine_table, sine_values = rope_tables(global_pos - sequence_start, HEAD_DIM)
    tok_f32 = tokens.astype(f32)
    scale_one = lax.rsqrt(jnp.mean(tok_f32 * tok_f32, axis=-1, keepdims=True) + norm_eps)
    unit_one = dot(tokens, shuffle, ((1,), (0,))) * scale_one
    gain_col = q_width + 2 * kv_width
    gain_one = jnp.concatenate([piece[:, gain_col] for piece in qkv_pieces]).astype(f32)[None, :]
    first_normed = (unit_one * gain_one).astype(bf16)
    projected = sum(
        dot(first_normed[:, i * piece.shape[0] : (i + 1) * piece.shape[0]], piece, ((1,), (0,)))
        for i, piece in enumerate(qkv_pieces)
    )
    query_rows = apply_rotation(
        projected[:, :q_width].reshape(tok_rows, QUERY_HEADS, HEAD_DIM), cosine_table, sine_values
    ).astype(bf16)
    key_rows = apply_rotation(
        projected[:, q_width : q_width + kv_width].reshape(tok_rows, KEY_HEADS, HEAD_DIM),
        cosine_table,
        sine_values,
    ).astype(bf16)
    value_rows = projected[:, q_width + kv_width : q_width + 2 * kv_width].astype(bf16)
    kv_rows = jnp.concatenate([key_rows.reshape(tok_rows, kv_width), value_rows], axis=1)
    kv_all = jnp.concatenate(gather_rows(kv_rows, 1), axis=0)
    shard = jnp.arange(fsdp_count, dtype=jnp.int32)
    shard_dev = (2 * (shard % chips) + shard // chips) ^ fsdp_at
    key_pos = (shard_dev[:, None] * tok_rows + token_index[None, :]).reshape(-1)
    allowed = (key_pos[None, :] <= global_pos[:, None]) & (
        key_pos[None, :] >= sequence_start[:, None]
    )
    keys = kv_all[:, :kv_width].reshape(-1, KEY_HEADS, HEAD_DIM)
    vals = kv_all[:, kv_width:].reshape(-1, KEY_HEADS, HEAD_DIM)
    grouped = query_rows.reshape(tok_rows, KEY_HEADS, heads_per_key, HEAD_DIM)
    mask = allowed[None, None]
    scores = (
        jnp.einsum("tgrd,kgd->grtk", grouped, keys, preferred_element_type=f32) * score_scale
    )
    row_max = jnp.max(jnp.where(mask, scores, masked_low), axis=-1, keepdims=True)
    summed = jnp.sum(jnp.where(mask, jnp.exp(scores - row_max), 0.0), axis=-1, keepdims=True)
    lse = row_max + jnp.log(summed)
    probs = jnp.where(mask, jnp.exp(scores - lse), 0.0)
    probs_b = probs.astype(bf16)
    attended = jnp.einsum("grtk,kgd->tgrd", probs_b, vals, preferred_element_type=f32).astype(bf16)
    attended_rows = attended.reshape(tok_rows, q_width)
    attended_rel = dot(attended_rows, shuffle, ((1,), (0,))).astype(bf16)
    hidden = tok_f32 + (
        dot(attended_rel[:, :half_width], output_own[:, :width], ((1,), (0,)))
        + dot(attended_rel[:, half_width:], output_other[:, :width], ((1,), (0,)))
    )
    scale_two = lax.rsqrt(jnp.mean(hidden * hidden, axis=-1, keepdims=True) + norm_eps)
    unit_two = hidden * scale_two
    normed_two = (unit_two * gain_two).astype(bf16)

    normed_pool = gather_pieces(normed_two, planes)
    win = jnp.zeros((held, width, ff_two), bf16)
    for k in range(dp_count):
        win = lax.dynamic_update_slice(win, in_parts[k], (0, (dp_at ^ k) * slice_width, 0))
    wout = jnp.concatenate(ordered(out_parts, dp_at), axis=2)
    expert_axis = jnp.arange(experts_total, dtype=jnp.int32)
    first_expert = fsdp_at * local_experts + group_at * held
    my_experts = first_expert + jnp.arange(held, dtype=jnp.int32)
    lower = (token_index[:, None] > token_index[None, :]).astype(bf16)

    def dense_gates(rows, chosen):
        logits = dot(rows, router_w, ((1,), (0,)))
        top = jnp.max(jnp.where(chosen, logits, masked_low), axis=-1, keepdims=True)
        raised = jnp.where(chosen, jnp.exp(logits - top), 0.0)
        return raised / jnp.sum(raised, axis=-1, keepdims=True)

    def chosen_of(ids):
        return jnp.any(ids[:, :, None] == expert_axis[None, None, :], axis=1)

    pieces = len(normed_pool)
    ids_all = jnp.stack([x[:, width : width + expert_ids.shape[1]] for x in d_pool])
    ids_all = ids_all.astype(jnp.int32)
    chosen_rows = (
        jnp.any(ids_all[:, None] == expert_axis[None, :, None, None], axis=-1).astype(f32)
    )
    mine = jnp.any(ids_all[:, None] == my_experts[None, :, None, None], axis=-1)
    mine = mine.reshape(pieces, held, planes, tok_rows)
    before = jnp.einsum(
        "iepu,tu->iept", mine.astype(bf16), lower, preferred_element_type=f32
    ).astype(jnp.int32)
    slots = jnp.where(mine, before, -1).transpose(0, 2, 1, 3).reshape(-1, held, tok_rows)
    run = expert_kernel(pieces, planes, held, tok_rows, width, ff, experts_total)
    back_own, back_other, mix_own, mix_other, grad_in_b, grad_out_b = run(
        first_expert[None], router_w.T, chosen_rows, slots, win, wout, *normed_pool, *d_pool
    )
    back = scatter_all(back_own, back_other, tok_rows, planes)

    in_sent, out_sent = [], []
    for k in range(dp_count):
        target = dp_at ^ k
        in_piece = lax.dynamic_slice_in_dim(grad_in_b, target * slice_width, slice_width, 1)
        out_piece = lax.dynamic_slice_in_dim(grad_out_b, target * slice_width, slice_width, 2)
        if k:
            in_piece, out_piece = swap(in_piece, "dp", k), swap(out_piece, "dp", k)
        in_sent.append(in_piece)
        out_sent.append(out_piece)

    d_block = d_out.astype(f32)
    d_gate = (
        back[:, width : width + experts_total]
        + back[:, width + experts_total : width + 2 * experts_total]
    )
    gates = dense_gates(normed_two, chosen_of(expert_ids))
    d_logits = (gates * (d_gate - jnp.sum(gates * d_gate, axis=-1, keepdims=True))).astype(bf16)
    d_normed_two = back[:, :width] + dot(d_logits, router_w, ((1,), (1,)))
    d_hidden_two, grad_gain_two = norm_backward(d_normed_two, unit_two, scale_two, gain_two)
    d_hidden = d_block + d_hidden_two
    d_hidden_b = d_hidden.astype(bf16)
    normed_two_rel = dot(normed_two, shuffle, ((1,), (0,))).astype(bf16)
    gain_two_rel = jnp.dot(
        grad_gain_two[None, :], shuffle.astype(f32), precision=lax.Precision.HIGHEST
    )[0]
    grad_output_own = dot(attended_rel[:, :half_width], d_hidden_b, ((0,), (0,)))
    grad_output_other = dot(attended_rel[:, half_width:], d_hidden_b, ((0,), (0,))).astype(bf16)
    grad_router_rel = dot(normed_two_rel, d_logits, ((0,), (0,)))

    grad_attended_rel = jnp.concatenate(
        [
            dot(d_hidden_b, output_own[:, :width], ((1,), (1,))),
            dot(d_hidden_b, output_other[:, :width], ((1,), (1,))),
        ],
        axis=1,
    ).astype(bf16)
    grad_attended = dot(grad_attended_rel, shuffle, ((1,), (1,))).astype(bf16)
    grad_grouped = grad_attended.reshape(tok_rows, KEY_HEADS, heads_per_key, HEAD_DIM)
    delta = jnp.sum(grad_grouped.astype(f32) * attended.astype(f32), axis=-1).transpose(1, 2, 0)
    d_vals = jnp.einsum("grtk,tgrd->kgd", probs_b, grad_grouped, preferred_element_type=f32)
    d_probs = jnp.einsum("tgrd,kgd->grtk", grad_grouped, vals, preferred_element_type=f32)
    d_scores = (probs * (d_probs - delta[..., None]) * score_scale).astype(bf16)
    d_queries = jnp.einsum("grtk,kgd->tgrd", d_scores, keys, preferred_element_type=f32)
    d_keys = jnp.einsum("grtk,tgrd->kgd", d_scores, grouped, preferred_element_type=f32)
    d_kv = jnp.concatenate([d_keys.reshape(-1, kv_width), d_vals.reshape(-1, kv_width)], axis=1)
    split_at = chips * tok_rows
    d_kv_own = scatter_chips(d_kv[:split_at], d_kv[split_at:].astype(bf16), tok_rows)
    summed_output = scatter_all(grad_output_own, grad_output_other, own_rows, dp_count)
    d_query_b = apply_rotation(
        d_queries.reshape(tok_rows, QUERY_HEADS, HEAD_DIM), cosine_table, -sine_values
    ).astype(bf16)
    d_key_b = apply_rotation(
        d_kv_own[:, :kv_width].reshape(tok_rows, KEY_HEADS, HEAD_DIM), cosine_table, -sine_values
    ).astype(bf16)
    d_proj = jnp.concatenate(
        [
            d_query_b.reshape(tok_rows, q_width),
            d_key_b.reshape(tok_rows, kv_width),
            d_kv_own[:, kv_width:].astype(bf16),
        ],
        axis=1,
    )
    qkv_all = jnp.concatenate(qkv_pieces, axis=0)
    d_normed_one = dot(d_proj, qkv_all[:, :gain_col], ((1,), (1,)))
    d_tok_rel, grad_gain_one = norm_backward(d_normed_one, unit_one, scale_one, gain_one)
    high = d_tok_rel.astype(bf16)
    low = (d_tok_rel - high.astype(f32)).astype(bf16)
    d_tokens = d_hidden + dot(high, shuffle, ((1,), (1,))) + dot(low, shuffle, ((1,), (1,)))
    grad_small = jnp.concatenate(
        [
            grad_router_rel,
            grad_gain_one[:, None],
            gain_two_rel[:, None],
            jnp.zeros((width, PAD - experts_total - 2), f32),
        ],
        axis=1,
    )
    summed_qkv = scatter_all(
        dot(first_normed[:, :half_width], d_proj, ((0,), (0,))),
        dot(first_normed[:, half_width:], d_proj, ((0,), (0,))).astype(bf16),
        own_rows,
        dp_count,
    )
    summed_small = scatter_all(grad_small[:half_width], grad_small[half_width:], own_rows, dp_count)

    mixture = scatter_all(mix_own, mix_other, tok_rows, planes, (grad_attended, d_proj))
    block_out = (hidden + mixture).astype(bf16)

    in_sent, out_sent = after((in_sent, out_sent), d_proj)
    in_back, out_back = [None] * planes, [None] * planes
    for k in range(dp_count):
        j = k % planes
        for back_list, sent in ((in_back, in_sent), (out_back, out_sent)):
            piece = sent[k].astype(f32)
            back_list[j] = piece if back_list[j] is None else back_list[j] + piece
    d_expert_in = jnp.concatenate(ordered(in_back, group_at), axis=0)
    d_expert_out = jnp.concatenate(ordered(out_back, group_at), axis=0)
    return (
        block_out,
        d_tokens,
        summed_small[:, experts_total],
        summed_qkv[:, :q_width],
        summed_qkv[:, q_width : q_width + kv_width],
        summed_qkv[:, q_width + kv_width : gain_col],
        summed_output,
        summed_small[:, experts_total + 1],
        summed_small[:, :experts_total],
        d_expert_in,
        d_expert_out,
    )


def solution(mesh):
    in_specs = (
        P(("dp", "fsdp"), None),
        P("dp", None),
        P(("dp", "fsdp"), None),
        P(("dp", "fsdp")),
        P(("dp", "fsdp"), None),
        P(("dp", "fsdp"), None),
        P(("dp", "fsdp"), None),
        P(("dp", "fsdp"), None),
        P(("dp", "fsdp")),
        P(("dp", "fsdp"), None),
        P("fsdp", "dp", None),
        P("fsdp", None, "dp"),
        P(("dp", "fsdp"), None),
    )
    out_specs = (
        P(("dp", "fsdp"), None),
        P(("dp", "fsdp"), None),
        P(("dp", "fsdp")),
        P(("dp", "fsdp"), None),
        P(("dp", "fsdp"), None),
        P(("dp", "fsdp"), None),
        P(("dp", "fsdp"), None),
        P(("dp", "fsdp")),
        P(("dp", "fsdp"), None),
        P("fsdp", "dp", None),
        P("fsdp", None, "dp"),
    )
    return jax.shard_map(local, mesh=mesh, in_specs=in_specs, out_specs=out_specs, check_vma=False)
```

time: 1670 us -> 647 us (0.39)
  waiting for transfers between devices: 1260 us -> 300 us
  blocking collectives: 156 us -> 0 us
  starting transfers between devices: 18.7 us -> 124 us
  matrix products: 96.4 us -> 52 us
  Pallas kernels: 0 us -> 30.8 us
    reduce_scatter x7 -> x0, waiting for transfers between devices: 855 us -> none  [the longest x1 145 us: local(): lax.psum_scatter(grad_in_local.astype(jnp.bfloat16), 'dp', scatter_dimens...]
    all_gather x8 -> x0, waiting for transfers between devices: 304 us -> none  [the longest x1 70.9 us: local(): lax.all_gather(expert_out, 'dp', axis=2, tiled=True)]
    ppermute x0 -> x84, waiting for transfers between devices: none -> 300 us  [swap(): return lax.ppermute(values, axis, [(i, i ^ mask) for i in range(count)])]
    ppermute x0 -> x84, starting transfers between devices: none -> 124 us  [swap(): return lax.ppermute(values, axis, [(i, i ^ mask) for i in range(count)])]
    unnamed x2 -> x0, blocking collectives: 85.6 us -> none
    all_gather x1 -> x0, blocking collectives: 70.7 us -> none  [local(): lax.all_gather(w_router, ('dp', 'fsdp'), axis=0, tiled=True)]
    all_to_all x4 -> x0, waiting for transfers between devices: 53.3 us -> none  [the longest x1 29.3 us: local(): lax.all_to_all(d_rows, 'fsdp', split_axis=1, concat_axis=1, tiled=True)]
    unnamed x19 -> x0, waiting for transfers between devices: 46.3 us -> none
  transfers between devices with their start and end apart: 21 -> 84, of which waited for: 19 -> 26; matrix products, arithmetic and copies ran while one was open for 9% -> 27% of each run, Pallas kernels for 0% -> 0%
where the time goes in v1:
time: 647 us; the launch traced here: 642 us
  waiting for transfers between devices  300 us (46%)
  starting transfers between devices  124 us (19%)
  local copies, waits for them, and re-layouts  80.8 us (12%)
  matrix products  52 us (8%)
  other arithmetic  51 us (8%)
  Pallas kernels  30.8 us (5%)
    ppermute x84, waiting for transfers between devices, swap(): return lax.ppermute(values, axis, [(i, i ^ mask) for i in range(count)])  300 us
    ppermute x84, starting transfers between devices, swap(): return lax.ppermute(values, axis, [(i, i ^ mask) for i in range(count)])  124 us
    dot_general x27, matrix products, dot(): lax.dot_general(left, right, (dims, ((), ())), preferred_element_type=f32)  32.9 us
    pallas_call x1, Pallas kernels, local(): run(first_expert[None], router_w.T, chosen_rows, slots, win, wout, *norme...  30.8 us
    unnamed x219, local copies, waits for them, and re-layouts  27.2 us
  transfers between devices with their start and end apart: 84, of which 26 were waited for; matrix products, arithmetic and copies ran while one was open for 27% of the time, Pallas kernels for 0%

profile of v1, /device:TPU:0, one launch (start us, length us, event | category | flops | bytes accessed | tf_op | source)
XLA Modules:
  0.0 641.7 jit_solution(3881457685307550230)
XLA Ops:
  2.3 3.1 collective-permute-start.14
  5.4 2.6 collective-permute-start.15
  9.8 3.9 collective-permute-start.2
  24.1 2.3 dynamic-slice_bitcast_fusion
  27.3 2.5 broadcast_in_dim.115
  35.0 3.7 collective-permute-start.32
  48.1 29.0 %collective-permute-done.21 = bf16[128,1152]{1,0:T(8,128)(2,1)S(1)} collective-permute-done((bf16[128,1152]{1,0:T(8,128)(2,1)S(1)}, bf16[128,1152]{1,0:T(8,128)(2,1)S(1)}, u32[]{:S(2)}, u32[]{:S(2)}) %collective-permute-start.21) | collective-permute-done | bytes 294944 | tf_op jit(solution)/shard_map/ppermute | solution.py:31
  81.8 9.5 %collective-permute-done.18 = bf16[128,1152]{1,0:T(8,128)(2,1)S(1)} collective-permute-done((bf16[128,1152]{1,0:T(8,128)(2,1)S(1)}, bf16[128,1152]{1,0:T(8,128)(2,1)S(1)}, u32[]{:S(2)}, u32[]{:S(2)}) %collective-permute-start.18) | collective-permute-done | bytes 294944 | tf_op jit(solution)/shard_map/ppermute | solution.py:31
  91.3 2.4 collective-permute-start.5
  100.9 19.0 %collective-permute-done.3 = bf16[128,2176]{1,0:T(8,128)(2,1)S(1)} collective-permute-done((bf16[128,2176]{1,0:T(8,128)(2,1)}, bf16[128,2176]{1,0:T(8,128)(2,1)S(1)}, u32[]{:S(2)}, u32[]{:S(2)}) %collective-permute-start.3) | collective-permute-done | bytes 557088 | tf_op jit(solution)/shard_map/ppermute | solution.py:31
  120.7 2.5 collective-permute-start.30
  123.4 2.5 collective-permute-start.24
  126.8 5.8 collective-permute-done.22.refs_15_
  133.5 9.1 %collective-permute-done.23.refs_16_ = bf16[256,1152]{1,0:T(8,128)(2,1)S(1)} collective-permute-done((bf16[256,1152]{1,0:T(8,128)(2,1)}, bf16[256,1152]{1,0:T(8,128)(2,1)S(1)}, u32[]{:S(2)}, u32[]{:S(2)}) %collective-permute-start.23) | collective-permute-done | bytes 589856 | tf_op jit(solution)/shard_map/ppermute | solution.py:31
  146.5 17.8 %collective-permute-done.29 = bf16[2,256,1024]{2,1,0:T(8,128)(2,1)} collective-permute-done((bf16[2,256,1024]{2,1,0:T(8,128)(2,1)}, bf16[2,256,1024]{2,1,0:T(8,128)(2,1)}, u32[]{:S(2)}, u32[]{:S(2)}) %collective-permute-start.29) | collective-permute-done | bytes 1048608 | tf_op jit(solution)/shard_map/ppermute | solution.py:31
  165.8 2.3 constant_dynamic-update-slice_fusion.33
  168.2 2.3 constant_dynamic-update-slice_fusion.32
  184.6 5.9 collective-permute-done.31
  190.5 2.4 collective-permute-start.12
  192.9 2.3 constant_dynamic-update-slice_fusion.31.refs_4_
  213.0 2.4 fusion.3
  224.8 21.8 %collective-permute-start.35 = (bf16[128,1024]{1,0:T(8,128)(2,1)S(1)}, bf16[128,1024]{1,0:T(8,128)(2,1)S(1)}, u32[]{:S(2)}, u32[]{:S(2)}) collective-permute-start(bf16[128,1024]{1,0:T(8,128)(2,1)S(1)} %multiply_convert_fusion), channel_id=1, source_target_pairs={{0,8},{8,0},{16,24},{24,16},{1,9},{9,1},{17,25},{25,17},{2,10},{10... | collective-permute-start | bytes 786440 | tf_op jit(solution)/shard_map/ppermute | solution.py:31
  248.3 5.3 collective-permute-done.35
  263.0 6.5 %collective-permute-done.36.refs_7_ = bf16[256,1024]{1,0:T(8,128)(2,1)} collective-permute-done((bf16[256,1024]{1,0:T(8,128)(2,1)}, bf16[256,1024]{1,0:T(8,128)(2,1)}, u32[]{:S(2)}, u32[]{:S(2)}) %collective-permute-start.36) | collective-permute-done | bytes 524320 | tf_op jit(solution)/shard_map/ppermute | solution.py:31
  269.5 11.4 %collective-permute-done.37.refs_8_ = bf16[256,1024]{1,0:T(8,128)(2,1)} collective-permute-done((bf16[256,1024]{1,0:T(8,128)(2,1)}, bf16[256,1024]{1,0:T(8,128)(2,1)}, u32[]{:S(2)}, u32[]{:S(2)}) %collective-permute-start.37) | collective-permute-done | bytes 524320 | tf_op jit(solution)/shard_map/ppermute | solution.py:31
  285.8 30.8 %experts.1 = (bf16[1024,1152]{1,0:T(8,128)(2,1)}, bf16[1024,1152]{1,0:T(8,128)(2,1)}, bf16[1024,1024]{1,0:T(8,128)(2,1)}, bf16[1024,1024]{1,0:T(8,128)(2,1)}, bf...) custom-call(s32[1]{0:T(128)} %bitcast.20.refs_0_, bf16[32,1024]{1,0:T(8,128)(2,1)} %slice_bitcast_fusion.7.refs_1_, ...), custom_call_target="tpu_custom_call" | custom-call | tf_op jit(solution)/shard_map/experts/pallas_call | solution.py:413
  326.4 2.9 fusion.180
  335.1 4.7 constant_dynamic-slice_fusion.4
  342.7 5.0 collective-permute-done.48
  349.2 10.2 %collective-permute-done.47 = bf16[256,1152]{1,0:T(8,128)(2,1)} collective-permute-done((bf16[256,1152]{1,0:T(8,128)(2,1)S(1)}, bf16[256,1152]{1,0:T(8,128)(2,1)}, u32[]{:S(2)}, u32[]{:S(2)}) %collective-permute-start.47) | collective-permute-done | bytes 589856 | tf_op jit(solution)/shard_map/ppermute | solution.py:31
  363.2 4.7 fusion.179
  371.6 10.2 %collective-permute-done.49 = bf16[128,1152]{1,0:T(8,128)(2,1)S(1)} collective-permute-done((bf16[128,1152]{1,0:T(8,128)(2,1)S(1)}, bf16[128,1152]{1,0:T(8,128)(2,1)S(1)}, u32[]{:S(2)}, u32[]{:S(2)}) %collective-permute-start.49) | collective-permute-done | bytes 294944 | tf_op jit(solution)/shard_map/ppermute | solution.py:31
  390.2 4.8 collective-permute-done.50
  399.5 5.2 fusion.125
  404.8 3.4 fusion.2
  412.9 4.2 fusion.43
  427.5 4.0 collective-permute-done.56
  433.0 4.1 collective-permute-done.55
  444.2 3.4 collective-permute-done.73
  455.0 41.0 %collective-permute-done.52 = bf16[128,1024]{1,0:T(8,128)(2,1)S(1)} collective-permute-done((bf16[128,1024]{1,0:T(8,128)(2,1)S(1)}, bf16[128,1024]{1,0:T(8,128)(2,1)S(1)}, u32[]{:S(2)}, u32[]{:S(2)}) %collective-permute-start.52) | collective-permute-done | bytes 262176 | tf_op jit(solution)/shard_map/ppermute | solution.py:31
  498.4 70.2 %collective-permute-done.82 = bf16[2,512,256]{2,1,0:T(8,128)(2,1)S(1)} collective-permute-done((bf16[2,512,256]{2,1,0:T(8,128)(2,1)S(1)}, bf16[2,512,256]{2,1,0:T(8,128)(2,1)S(1)}, u32[]{:S(2)}, u32[]{:S(2)}) %collective-permute-start.82) | collective-permute-done | bytes 524320 | tf_op jit(solution)/shard_map/ppermute | solution.py:31
  571.3 11.9 %collective-permute-start.76 = (bf16[32,1024]{1,0:T(8,128)(2,1)S(1)}, bf16[32,1024]{1,0:T(8,128)(2,1)S(1)}, u32[]{:S(2)}, u32[]{:S(2)}) collective-permute-start(bf16[32,1024]{1,0:T(8,128)(2,1)S(1)} %get-tuple-element.119), channel_id=1, source_target_pairs={{0,16},{8,24},{16,0},{24,8},{1,17},{9,25},{17,1},{25,9},{2,18},{10... | collective-permute-start | bytes 196616 | tf_op jit(solution)/shard_map/ppermute | solution.py:31
  585.5 2.8 pad_maximum_fusion
  604.0 2.2 collective-permute-start.63
  607.6 7.9 %collective-permute-done.67 = bf16[128,2048]{1,0:T(8,128)(2,1)S(1)} collective-permute-done((bf16[128,2048]{1,0:T(8,128)(2,1)S(1)}, bf16[128,2048]{1,0:T(8,128)(2,1)S(1)}, u32[]{:S(2)}, u32[]{:S(2)}) %collective-permute-start.67) | collective-permute-done | bytes 524320 | tf_op jit(solution)/shard_map/ppermute | solution.py:31
  617.5 7.3 %collective-permute-done.66 = bf16[128,2048]{1,0:T(8,128)(2,1)S(1)} collective-permute-done((bf16[128,2048]{1,0:T(8,128)(2,1)S(1)}, bf16[128,2048]{1,0:T(8,128)(2,1)S(1)}, u32[]{:S(2)}, u32[]{:S(2)}) %collective-permute-start.66) | collective-permute-done | bytes 524320 | tf_op jit(solution)/shard_map/ppermute | solution.py:31
  630.4 3.1 collective-permute-done.70
  633.5 6.5 %collective-permute-done.69 = bf16[32,2048]{1,0:T(8,128)(2,1)S(1)} collective-permute-done((bf16[32,2048]{1,0:T(8,128)(2,1)S(1)}, bf16[32,2048]{1,0:T(8,128)(2,1)S(1)}, u32[]{:S(2)}, u32[]{:S(2)}) %collective-permute-start.69) | collective-permute-done | bytes 131104 | tf_op jit(solution)/shard_map/ppermute | solution.py:31
  (526 shorter events, 210.0 us)
Async XLA Ops:
  2.3 31.4 %collective-permute-start.14 = (bf16[32,1152]{1,0:T(8,128)(2,1)S(1)}, bf16[32,1152]{1,0:T(8,128)(2,1)S(1)}, u32[]{:S(2)}, u32[]{:S(2)}) collective-permute-start(bf16[32,1152]{1,0:T(8,128)(2,1)S(1)} %concatenate.127), channel_id=1, source_target_pairs={{0,8},{8,0},{16,24},{24,16},{1,9},{9,1},{17,25},{25,17},{2,10},{10... | collective-permute-start | bytes 221192 | tf_op jit(solution)/shard_map/ppermute | solution.py:31
  5.4 29.5 %collective-permute-start.15 = (bf16[32,1152]{1,0:T(8,128)(2,1)S(1)}, bf16[32,1152]{1,0:T(8,128)(2,1)S(1)}, u32[]{:S(2)}, u32[]{:S(2)}) collective-permute-start(bf16[32,1152]{1,0:T(8,128)(2,1)S(1)} %concatenate.127), channel_id=1, source_target_pairs={{0,16},{8,24},{16,0},{24,8},{1,17},{9,25},{17,1},{25,9},{2,18},{10... | collective-permute-start | bytes 221192 | tf_op jit(solution)/shard_map/ppermute | solution.py:31
  8.0 31.3 %collective-permute-start.16 = (bf16[32,1152]{1,0:T(8,128)(2,1)S(1)}, bf16[32,1152]{1,0:T(8,128)(2,1)S(1)}, u32[]{:S(2)}, u32[]{:S(2)}) collective-permute-start(bf16[32,1152]{1,0:T(8,128)(2,1)S(1)} %concatenate.127), channel_id=1, source_target_pairs={{0,24},{8,16},{16,8},{24,0},{1,25},{9,17},{17,9},{25,1},{2,26},{10... | collective-permute-start | bytes 221192 | tf_op jit(solution)/shard_map/ppermute | solution.py:31
  9.8 30.3 %collective-permute-start.2 = (bf16[32,2176]{1,0:T(8,128)(2,1)S(1)}, bf16[32,2176]{1,0:T(8,128)(2,1)S(1)}, u32[]{:S(2)}, u32[]{:S(2)}) collective-permute-start(bf16[32,2176]{1,0:T(8,128)(2,1)S(1)} %concatenate.109), channel_id=1, source_target_pairs={{0,24},{8,16},{16,8},{24,0},{1,25},{9,17},{17,9},{25,1},{2,26},{10... | collective-permute-start | bytes 417800 | tf_op jit(solution)/shard_map/ppermute | solution.py:31
  13.6 28.4 %collective-permute-start.1 = (bf16[32,2176]{1,0:T(8,128)(2,1)S(1)}, bf16[32,2176]{1,0:T(8,128)(2,1)S(1)}, u32[]{:S(2)}, u32[]{:S(2)}) collective-permute-start(bf16[32,2176]{1,0:T(8,128)(2,1)S(1)} %concatenate.109), channel_id=1, source_target_pairs={{0,16},{8,24},{16,0},{24,8},{1,17},{9,25},{17,1},{25,9},{2,18},{10... | collective-permute-start | bytes 417800 | tf_op jit(solution)/shard_map/ppermute | solution.py:31
  35.0 60.7 %collective-permute-start.32 = (bf16[2,512,256]{2,1,0:T(8,128)(2,1)}, bf16[2,512,256]{2,1,0:T(8,128)(2,1)}, u32[]{:S(2)}, u32[]{:S(2)}) collective-permute-start(bf16[2,512,256]{2,1,0:T(8,128)(2,1)} %get-tuple-element.104), channel_id=1, source_target_pairs={{0,24},{8,16},{16,8},{24,0},{1,25},{9,17},{17,9},{25,1},{2,26},{10... | collective-permute-start | bytes 1572872 | tf_op jit(solution)/shard_map/ppermute | solution.py:31
  39.4 56.9 %collective-permute-start.34 = (bf16[2,512,256]{2,1,0:T(8,128)(2,1)}, bf16[2,512,256]{2,1,0:T(8,128)(2,1)}, u32[]{:S(2)}, u32[]{:S(2)}) collective-permute-start(bf16[2,512,256]{2,1,0:T(8,128)(2,1)} %get-tuple-element.104), channel_id=1, source_target_pairs={{0,8},{8,0},{16,24},{24,16},{1,9},{9,1},{17,25},{25,17},{2,10},{10... | collective-permute-start | bytes 1572872 | tf_op jit(solution)/shard_map/ppermute | solution.py:31
  40.0 37.1 %collective-permute-start.21 = (bf16[128,1152]{1,0:T(8,128)(2,1)S(1)}, bf16[128,1152]{1,0:T(8,128)(2,1)S(1)}, u32[]{:S(2)}, u32[]{:S(2)}) collective-permute-start(bf16[128,1152]{1,0:T(8,128)(2,1)S(1)} %concatenate.130), channel_id=1, source_target_pairs={{0,8},{8,0},{16,24},{24,16},{1,9},{9,1},{17,25},{25,17},{2,10},{10... | collective-permute-start | bytes 884744 | tf_op jit(solution)/shard_map/ppermute | solution.py:31
  42.1 54.2 %collective-permute-start.33 = (bf16[2,512,256]{2,1,0:T(8,128)(2,1)S(1)}, bf16[2,512,256]{2,1,0:T(8,128)(2,1)}, u32[]{:S(2)}, u32[]{:S(2)}) collective-permute-start(bf16[2,512,256]{2,1,0:T(8,128)(2,1)S(1)} %get-tuple-element.105), channel_id=1, source_target_pairs={{0,16},{8,24},{16,0},{24,8},{1,17},{9,25},{17,1},{25,9},{2,18},{10... | collective-permute-start | bytes 1572872 | tf_op jit(solution)/shard_map/ppermute | solution.py:31
  42.1 37.5 %collective-permute-start.17 = (bf16[128,1152]{1,0:T(8,128)(2,1)S(1)}, bf16[128,1152]{1,0:T(8,128)(2,1)S(1)}, u32[]{:S(2)}, u32[]{:S(2)}) collective-permute-start(bf16[128,1152]{1,0:T(8,128)(2,1)S(1)} %pad_maximum_fusion.9), channel_id=1, source_target_pairs={{0,2},{1,3},{2,0},{3,1},{4,6},{5,7},{6,4},{7,5},{8,10},{9,11},{10,... | collective-permute-start | bytes 884744 | tf_op jit(solution)/shard_map/ppermute | solution.py:31
  91.3 29.5 %collective-permute-start.5 = (bf16[128,2176]{1,0:T(8,128)(2,1)}, bf16[128,2176]{1,0:T(8,128)(2,1)S(1)}, u32[]{:S(2)}, u32[]{:S(2)}) collective-permute-start(bf16[128,2176]{1,0:T(8,128)(2,1)} %pad_maximum_fusion.6), channel_id=1, source_target_pairs={{0,6},{1,7},{2,4},{3,5},{4,2},{5,3},{6,0},{7,1},{8,14},{9,15},{10,... | collective-permute-start | bytes 1671176 | tf_op jit(solution)/shard_map/ppermute | solution.py:31
  94.5 25.5 %collective-permute-start.3 = (bf16[128,2176]{1,0:T(8,128)(2,1)}, bf16[128,2176]{1,0:T(8,128)(2,1)S(1)}, u32[]{:S(2)}, u32[]{:S(2)}) collective-permute-start(bf16[128,2176]{1,0:T(8,128)(2,1)} %pad_maximum_fusion.6), channel_id=1, source_target_pairs={{0,2},{1,3},{2,0},{3,1},{4,6},{5,7},{6,4},{7,5},{8,10},{9,11},{10,... | collective-permute-start | bytes 1671176 | tf_op jit(solution)/shard_map/ppermute | solution.py:31
  95.7 24.8 %collective-permute-start.4 = (bf16[128,2176]{1,0:T(8,128)(2,1)}, bf16[128,2176]{1,0:T(8,128)(2,1)S(1)}, u32[]{:S(2)}, u32[]{:S(2)}) collective-permute-start(bf16[128,2176]{1,0:T(8,128)(2,1)} %pad_maximum_fusion.6), channel_id=1, source_target_pairs={{0,4},{1,5},{2,6},{3,7},{4,0},{5,1},{6,2},{7,3},{8,12},{9,13},{10,... | collective-permute-start | bytes 1671176 | tf_op jit(solution)/shard_map/ppermute | solution.py:31
  96.2 27.1 %collective-permute-start.6 = (bf16[128,2176]{1,0:T(8,128)(2,1)}, bf16[128,2176]{1,0:T(8,128)(2,1)S(1)}, u32[]{:S(2)}, u32[]{:S(2)}) collective-permute-start(bf16[128,2176]{1,0:T(8,128)(2,1)} %pad_maximum_fusion.6), channel_id=1, source_target_pairs={{0,1},{1,0},{2,3},{3,2},{4,5},{5,4},{6,7},{7,6},{8,9},{9,8},{10,11... | collective-permute-start | bytes 1671176 | tf_op jit(solution)/shard_map/ppermute | solution.py:31
  96.2 36.4 %collective-permute-start.22 = (bf16[256,1152]{1,0:T(8,128)(2,1)}, bf16[256,1152]{1,0:T(8,128)(2,1)}, u32[]{:S(2)}, u32[]{:S(2)}) collective-permute-start(bf16[256,1152]{1,0:T(8,128)(2,1)} %pad_maximum_fusion.5.refs_14_), channel_id=1, source_target_pairs={{0,2},{1,3},{2,0},{3,1},{4,6},{5,7},{6,4},{7,5},{8,10},{9,11},{10,... | collective-permute-start | bytes 1769480 | tf_op jit(solution)/shard_map/ppermute | solution.py:31
  119.9 22.7 %collective-permute-start.23 = (bf16[256,1152]{1,0:T(8,128)(2,1)}, bf16[256,1152]{1,0:T(8,128)(2,1)S(1)}, u32[]{:S(2)}, u32[]{:S(2)}) collective-permute-start(bf16[256,1152]{1,0:T(8,128)(2,1)} %pad_maximum_fusion.5.refs_14_), channel_id=1, source_target_pairs={{0,4},{1,5},{2,6},{3,7},{4,0},{5,1},{6,2},{7,3},{8,12},{9,13},{10,... | collective-permute-start | bytes 1769480 | tf_op jit(solution)/shard_map/ppermute | solution.py:31
  120.5 43.8 %collective-permute-start.29 = (bf16[2,256,1024]{2,1,0:T(8,128)(2,1)}, bf16[2,256,1024]{2,1,0:T(8,128)(2,1)}, u32[]{:S(2)}, u32[]{:S(2)}) collective-permute-start(bf16[2,256,1024]{2,1,0:T(8,128)(2,1)} %dynamic-slice_bitcast_fusion), channel_id=1, source_target_pairs={{0,8},{8,0},{16,24},{24,16},{1,9},{9,1},{17,25},{25,17},{2,10},{10... | collective-permute-start | bytes 3145736 | tf_op jit(solution)/shard_map/ppermute | solution.py:31
  120.7 47.4 %collective-permute-start.30 = (bf16[2,256,1024]{2,1,0:T(8,128)(2,1)}, bf16[2,256,1024]{2,1,0:T(8,128)(2,1)}, u32[]{:S(2)}, u32[]{:S(2)}) collective-permute-start(bf16[2,256,1024]{2,1,0:T(8,128)(2,1)} %get-tuple-element.64), channel_id=1, source_target_pairs={{0,16},{8,24},{16,0},{24,8},{1,17},{9,25},{17,1},{25,9},{2,18},{10... | collective-permute-start | bytes 3145736 | tf_op jit(solution)/shard_map/ppermute | solution.py:31
  142.6 29.8 %collective-permute-start.9 = (bf16[128,2176]{1,0:T(8,128)(2,1)S(1)}, bf16[128,2176]{1,0:T(8,128)(2,1)}, u32[]{:S(2)}, u32[]{:S(2)}) collective-permute-start(bf16[128,2176]{1,0:T(8,128)(2,1)S(1)} %collective-permute-done.5), channel_id=1, source_target_pairs={{0,1},{1,0},{2,3},{3,2},{4,5},{5,4},{6,7},{7,6},{8,9},{9,8},{10,11... | collective-permute-start | bytes 1671176 | tf_op jit(solution)/shard_map/ppermute | solution.py:31
  143.4 27.0 %collective-permute-start.7 = (bf16[128,2176]{1,0:T(8,128)(2,1)S(1)}, bf16[128,2176]{1,0:T(8,128)(2,1)S(1)}, u32[]{:S(2)}, u32[]{:S(2)}) collective-permute-start(bf16[128,2176]{1,0:T(8,128)(2,1)S(1)} %collective-permute-done.3), channel_id=1, source_target_pairs={{0,1},{1,0},{2,3},{3,2},{4,5},{5,4},{6,7},{7,6},{8,9},{9,8},{10,11... | collective-permute-start | bytes 1671176 | tf_op jit(solution)/shard_map/ppermute | solution.py:31
  144.8 26.5 %collective-permute-start.8 = (bf16[128,2176]{1,0:T(8,128)(2,1)S(1)}, bf16[128,2176]{1,0:T(8,128)(2,1)}, u32[]{:S(2)}, u32[]{:S(2)}) collective-permute-start(bf16[128,2176]{1,0:T(8,128)(2,1)S(1)} %collective-permute-done.4), channel_id=1, source_target_pairs={{0,1},{1,0},{2,3},{3,2},{4,5},{5,4},{6,7},{7,6},{8,9},{9,8},{10,11... | collective-permute-start | bytes 1671176 | tf_op jit(solution)/shard_map/ppermute | solution.py:31
  164.4 26.1 %collective-permute-start.31 = (bf16[2,256,1024]{2,1,0:T(8,128)(2,1)}, bf16[2,256,1024]{2,1,0:T(8,128)(2,1)}, u32[]{:S(2)}, u32[]{:S(2)}) collective-permute-start(bf16[2,256,1024]{2,1,0:T(8,128)(2,1)} %dynamic-slice_bitcast_fusion), channel_id=1, source_target_pairs={{0,24},{8,16},{16,8},{24,0},{1,25},{9,17},{17,9},{25,1},{2,26},{10... | collective-permute-start | bytes 3145736 | tf_op jit(solution)/shard_map/ppermute | solution.py:31
  168.2 36.2 %collective-permute-start.20 = (bf16[512,1152]{1,0:T(8,128)(2,1)}, bf16[512,1152]{1,0:T(8,128)(2,1)}, u32[]{:S(2)}, u32[]{:S(2)}) collective-permute-start(bf16[512,1152]{1,0:T(8,128)(2,1)} %constant_dynamic-update-slice_fusion.5), channel_id=1, source_target_pairs={{0,1},{1,0},{2,3},{3,2},{4,5},{5,4},{6,7},{7,6},{8,9},{9,8},{10,11... | collective-permute-start | bytes 3538952 | tf_op jit(solution)/shard_map/ppermute | solution.py:31
  170.4 76.2 %collective-permute-start.26 = (bf16[256,1152]{1,0:T(8,128)(2,1)}, bf16[256,1152]{1,0:T(8,128)(2,1)}, u32[]{:S(2)}, u32[]{:S(2)}) collective-permute-start(bf16[256,1152]{1,0:T(8,128)(2,1)} %collective-permute-done.22.refs_15_), channel_id=1, source_target_pairs={{0,1},{1,0},{2,3},{3,2},{4,5},{5,4},{6,7},{7,6},{8,9},{9,8},{10,11... | collective-permute-start | bytes 1769480 | tf_op jit(solution)/shard_map/ppermute | solution.py:31
  196.2 51.3 %collective-permute-start.27 = (bf16[256,1152]{1,0:T(8,128)(2,1)}, bf16[256,1152]{1,0:T(8,128)(2,1)}, u32[]{:S(2)}, u32[]{:S(2)}) collective-permute-start(bf16[256,1152]{1,0:T(8,128)(2,1)} %copy-done.42), channel_id=1, source_target_pairs={{0,1},{1,0},{2,3},{3,2},{4,5},{5,4},{6,7},{7,6},{8,9},{9,8},{10,11... | collective-permute-start | bytes 1769480 | tf_op jit(solution)/shard_map/ppermute | solution.py:31
  196.2 61.7 %collective-permute-start.28 = (bf16[256,1152]{1,0:T(8,128)(2,1)}, bf16[256,1152]{1,0:T(8,128)(2,1)}, u32[]{:S(2)}, u32[]{:S(2)}) collective-permute-start(bf16[256,1152]{1,0:T(8,128)(2,1)} %collective-permute-done.24.refs_17_), channel_id=1, source_target_pairs={{0,1},{1,0},{2,3},{3,2},{4,5},{5,4},{6,7},{7,6},{8,9},{9,8},{10,11... | collective-permute-start | bytes 1769480 | tf_op jit(solution)/shard_map/ppermute | solution.py:31
  224.8 28.8 %collective-permute-start.35 = (bf16[128,1024]{1,0:T(8,128)(2,1)S(1)}, bf16[128,1024]{1,0:T(8,128)(2,1)S(1)}, u32[]{:S(2)}, u32[]{:S(2)}) collective-permute-start(bf16[128,1024]{1,0:T(8,128)(2,1)S(1)} %multiply_convert_fusion), channel_id=1, source_target_pairs={{0,8},{8,0},{16,24},{24,16},{1,9},{9,1},{17,25},{25,17},{2,10},{10... | collective-permute-start | bytes 786440 | tf_op jit(solution)/shard_map/ppermute | solution.py:31
  255.9 25.0 %collective-permute-start.37 = (bf16[256,1024]{1,0:T(8,128)(2,1)}, bf16[256,1024]{1,0:T(8,128)(2,1)}, u32[]{:S(2)}, u32[]{:S(2)}) collective-permute-start(bf16[256,1024]{1,0:T(8,128)(2,1)} %pad_maximum_fusion.7.refs_6_), channel_id=1, source_target_pairs={{0,4},{1,5},{2,6},{3,7},{4,0},{5,1},{6,2},{7,3},{8,12},{9,13},{10,... | collective-permute-start | bytes 1572872 | tf_op jit(solution)/shard_map/ppermute | solution.py:31
  257.4 23.5 %collective-permute-start.38 = (bf16[256,1024]{1,0:T(8,128)(2,1)}, bf16[256,1024]{1,0:T(8,128)(2,1)}, u32[]{:S(2)}, u32[]{:S(2)}) collective-permute-start(bf16[256,1024]{1,0:T(8,128)(2,1)} %pad_maximum_fusion.7.refs_6_), channel_id=1, source_target_pairs={{0,6},{1,7},{2,4},{3,5},{4,2},{5,3},{6,0},{7,1},{8,14},{9,15},{10,... | collective-permute-start | bytes 1572872 | tf_op jit(solution)/shard_map/ppermute | solution.py:31
  325.9 37.3 %collective-permute-start.43 = (bf16[1024,1024]{1,0:T(8,128)(2,1)}, bf16[1024,1024]{1,0:T(8,128)(2,1)}, u32[]{:S(2)}, u32[]{:S(2)}) collective-permute-start(bf16[1024,1024]{1,0:T(8,128)(2,1)} %get-tuple-element.30), channel_id=1, source_target_pairs={{0,1},{1,0},{2,3},{3,2},{4,5},{5,4},{6,7},{7,6},{8,9},{9,8},{10,11... | collective-permute-start | bytes 6291464 | tf_op jit(solution)/shard_map/ppermute | solution.py:31
  331.7 27.6 %collective-permute-start.47 = (bf16[256,1152]{1,0:T(8,128)(2,1)S(1)}, bf16[256,1152]{1,0:T(8,128)(2,1)}, u32[]{:S(2)}, u32[]{:S(2)}) collective-permute-start(bf16[256,1152]{1,0:T(8,128)(2,1)S(1)} %get-tuple-element.79), channel_id=1, source_target_pairs={{0,4},{1,5},{2,6},{3,7},{4,0},{5,1},{6,2},{7,3},{8,12},{9,13},{10,... | collective-permute-start | bytes 1769480 | tf_op jit(solution)/shard_map/ppermute | solution.py:31
  332.4 27.0 %collective-permute-start.46 = (bf16[256,1152]{1,0:T(8,128)(2,1)S(1)}, bf16[256,1152]{1,0:T(8,128)(2,1)}, u32[]{:S(2)}, u32[]{:S(2)}) collective-permute-start(bf16[256,1152]{1,0:T(8,128)(2,1)S(1)} %get-tuple-element.77), channel_id=1, source_target_pairs={{0,2},{1,3},{2,0},{3,1},{4,6},{5,7},{6,4},{7,5},{8,10},{9,11},{10,... | collective-permute-start | bytes 1769480 | tf_op jit(solution)/shard_map/ppermute | solution.py:31
  339.8 229.3 %collective-permute-start.78 = (bf16[2,256,1024]{2,1,0:T(8,128)(2,1)}, bf16[2,256,1024]{2,1,0:T(8,128)(2,1)}, u32[]{:S(2)}, u32[]{:S(2)}) collective-permute-start(bf16[2,256,1024]{2,1,0:T(8,128)(2,1)} %get-tuple-element.73), channel_id=1, source_target_pairs={{0,8},{8,0},{16,24},{24,16},{1,9},{9,1},{17,25},{25,17},{2,10},{10... | collective-permute-start | bytes 3145736 | tf_op jit(solution)/shard_map/ppermute | solution.py:31
  347.7 105.0 %collective-permute-start.81 = (bf16[2,512,256]{2,1,0:T(8,128)(2,1)}, bf16[2,512,256]{2,1,0:T(8,128)(2,1)}, u32[]{:S(2)}, u32[]{:S(2)}) collective-permute-start(bf16[2,512,256]{2,1,0:T(8,128)(2,1)} %get-tuple-element.84), channel_id=1, source_target_pairs={{0,8},{8,0},{16,24},{24,16},{1,9},{9,1},{17,25},{25,17},{2,10},{10... | collective-permute-start | bytes 1572872 | tf_op jit(solution)/shard_map/ppermute | solution.py:31
  370.4 24.5 %collective-permute-start.50 = (bf16[256,1024]{1,0:T(8,128)(2,1)}, bf16[256,1024]{1,0:T(8,128)(2,1)}, u32[]{:S(2)}, u32[]{:S(2)}) collective-permute-start(bf16[256,1024]{1,0:T(8,128)(2,1)} %get-tuple-element.91), channel_id=1, source_target_pairs={{0,4},{1,5},{2,6},{3,7},{4,0},{5,1},{6,2},{7,3},{8,12},{9,13},{10,... | collective-permute-start | bytes 1572872 | tf_op jit(solution)/shard_map/ppermute | solution.py:31
  442.9 128.4 %collective-permute-start.79 = (bf16[2,256,1024]{2,1,0:T(8,128)(2,1)}, bf16[2,256,1024]{2,1,0:T(8,128)(2,1)S(1)}, u32[]{:S(2)}, u32[]{:S(2)}) collective-permute-start(bf16[2,256,1024]{2,1,0:T(8,128)(2,1)} %get-tuple-element.72), channel_id=1, source_target_pairs={{0,16},{8,24},{16,0},{24,8},{1,17},{9,25},{17,1},{25,9},{2,18},{10... | collective-permute-start | bytes 3145736 | tf_op jit(solution)/shard_map/ppermute | solution.py:31
  447.6 135.6 %collective-permute-start.80 = (bf16[2,256,1024]{2,1,0:T(8,128)(2,1)}, bf16[2,256,1024]{2,1,0:T(8,128)(2,1)S(1)}, u32[]{:S(2)}, u32[]{:S(2)}) collective-permute-start(bf16[2,256,1024]{2,1,0:T(8,128)(2,1)} %get-tuple-element.71), channel_id=1, source_target_pairs={{0,24},{8,16},{16,8},{24,0},{1,25},{9,17},{17,9},{25,1},{2,26},{10... | collective-permute-start | bytes 3145736 | tf_op jit(solution)/shard_map/ppermute | solution.py:31
  451.4 44.7 %collective-permute-start.52 = (bf16[128,1024]{1,0:T(8,128)(2,1)S(1)}, bf16[128,1024]{1,0:T(8,128)(2,1)S(1)}, u32[]{:S(2)}, u32[]{:S(2)}) collective-permute-start(bf16[128,1024]{1,0:T(8,128)(2,1)S(1)} %copy-done.51), channel_id=1, source_target_pairs={{0,8},{8,0},{16,24},{24,16},{1,9},{9,1},{17,25},{25,17},{2,10},{10... | collective-permute-start | bytes 786440 | tf_op jit(solution)/shard_map/ppermute | solution.py:31
  452.7 115.9 %collective-permute-start.82 = (bf16[2,512,256]{2,1,0:T(8,128)(2,1)S(1)}, bf16[2,512,256]{2,1,0:T(8,128)(2,1)S(1)}, u32[]{:S(2)}, u32[]{:S(2)}) collective-permute-start(bf16[2,512,256]{2,1,0:T(8,128)(2,1)S(1)} %copy-done.48), channel_id=1, source_target_pairs={{0,16},{8,24},{16,0},{24,8},{1,17},{9,25},{17,1},{25,9},{2,18},{10... | collective-permute-start | bytes 1572872 | tf_op jit(solution)/shard_map/ppermute | solution.py:31
  496.0 72.6 %collective-permute-start.83 = (bf16[2,512,256]{2,1,0:T(8,128)(2,1)S(1)}, bf16[2,512,256]{2,1,0:T(8,128)(2,1)S(1)}, u32[]{:S(2)}, u32[]{:S(2)}) collective-permute-start(bf16[2,512,256]{2,1,0:T(8,128)(2,1)S(1)} %copy-done.47), channel_id=1, source_target_pairs={{0,24},{8,16},{16,8},{24,0},{1,25},{9,17},{17,9},{25,1},{2,26},{10... | collective-permute-start | bytes 1572872 | tf_op jit(solution)/shard_map/ppermute | solution.py:31
  568.6 26.6 %collective-permute-start.57 = (bf16[512,128]{1,0:T(8,128)(2,1)S(1)}, bf16[512,128]{1,0:T(8,128)(2,1)S(1)}, u32[]{:S(2)}, u32[]{:S(2)}) collective-permute-start(bf16[512,128]{1,0:T(8,128)(2,1)S(1)} %slice.669), channel_id=1, source_target_pairs={{0,1},{1,0},{2,3},{3,2},{4,5},{5,4},{6,7},{7,6},{8,9},{9,8},{10,11... | collective-permute-start | bytes 393224 | tf_op jit(solution)/shard_map/ppermute | solution.py:31
  568.6 28.2 %collective-permute-start.64 = (bf16[512,2048]{1,0:T(8,128)(2,1)S(1)}, bf16[512,2048]{1,0:T(8,128)(2,1)S(1)}, u32[]{:S(2)}, u32[]{:S(2)}) collective-permute-start(bf16[512,2048]{1,0:T(8,128)(2,1)S(1)} %convolution_convert_fusion), channel_id=1, source_target_pairs={{0,1},{1,0},{2,3},{3,2},{4,5},{5,4},{6,7},{7,6},{8,9},{9,8},{10,11... | collective-permute-start | bytes 6291464 | tf_op jit(solution)/shard_map/ppermute | solution.py:31
  569.1 29.8 %collective-permute-start.77 = (bf16[32,1024]{1,0:T(8,128)(2,1)S(1)}, bf16[32,1024]{1,0:T(8,128)(2,1)S(1)}, u32[]{:S(2)}, u32[]{:S(2)}) collective-permute-start(bf16[32,1024]{1,0:T(8,128)(2,1)S(1)} %get-tuple-element.118), channel_id=1, source_target_pairs={{0,24},{8,16},{16,8},{24,0},{1,25},{9,17},{17,9},{25,1},{2,26},{10... | collective-permute-start | bytes 196616 | tf_op jit(solution)/shard_map/ppermute | solution.py:31
  571.3 28.5 %collective-permute-start.76 = (bf16[32,1024]{1,0:T(8,128)(2,1)S(1)}, bf16[32,1024]{1,0:T(8,128)(2,1)S(1)}, u32[]{:S(2)}, u32[]{:S(2)}) collective-permute-start(bf16[32,1024]{1,0:T(8,128)(2,1)S(1)} %get-tuple-element.119), channel_id=1, source_target_pairs={{0,16},{8,24},{16,0},{24,8},{1,17},{9,25},{17,1},{25,9},{2,18},{10... | collective-permute-start | bytes 196616 | tf_op jit(solution)/shard_map/ppermute | solution.py:31
  601.3 23.6 %collective-permute-start.66 = (bf16[128,2048]{1,0:T(8,128)(2,1)S(1)}, bf16[128,2048]{1,0:T(8,128)(2,1)S(1)}, u32[]{:S(2)}, u32[]{:S(2)}) collective-permute-start(bf16[128,2048]{1,0:T(8,128)(2,1)S(1)} %get-tuple-element.88), channel_id=1, source_target_pairs={{0,4},{1,5},{2,6},{3,7},{4,0},{5,1},{6,2},{7,3},{8,12},{9,13},{10,... | collective-permute-start | bytes 1572872 | tf_op jit(solution)/shard_map/ppermute | solution.py:31
  602.5 22.4 %collective-permute-start.65 = (bf16[128,2048]{1,0:T(8,128)(2,1)S(1)}, bf16[128,2048]{1,0:T(8,128)(2,1)S(1)}, u32[]{:S(2)}, u32[]{:S(2)}) collective-permute-start(bf16[128,2048]{1,0:T(8,128)(2,1)S(1)} %get-tuple-element.86), channel_id=1, source_target_pairs={{0,2},{1,3},{2,0},{3,1},{4,6},{5,7},{6,4},{7,5},{8,10},{9,11},{10,... | collective-permute-start | bytes 1572872 | tf_op jit(solution)/shard_map/ppermute | solution.py:31
  604.0 24.5 %collective-permute-start.63 = (bf16[32,128]{1,0:T(8,128)(2,1)S(1)}, bf16[32,128]{1,0:T(8,128)(2,1)S(1)}, u32[]{:S(2)}, u32[]{:S(2)}) collective-permute-start(bf16[32,128]{1,0:T(8,128)(2,1)S(1)} %get-tuple-element.128), channel_id=1, source_target_pairs={{0,24},{8,16},{16,8},{24,0},{1,25},{9,17},{17,9},{25,1},{2,26},{10... | collective-permute-start | bytes 24584 | tf_op jit(solution)/shard_map/ppermute | solution.py:31
  606.3 23.4 %collective-permute-start.62 = (bf16[32,128]{1,0:T(8,128)(2,1)S(1)}, bf16[32,128]{1,0:T(8,128)(2,1)S(1)}, u32[]{:S(2)}, u32[]{:S(2)}) collective-permute-start(bf16[32,128]{1,0:T(8,128)(2,1)S(1)} %get-tuple-element.129), channel_id=1, source_target_pairs={{0,16},{8,24},{16,0},{24,8},{1,17},{9,25},{17,1},{25,9},{2,18},{10... | collective-permute-start | bytes 24584 | tf_op jit(solution)/shard_map/ppermute | solution.py:31
  (129 other events, 1764.3 us)

commit v2 on v1

--- a/solution.py
+++ b/solution.py
@@ -12,6 +12,8 @@
 KEY_HEADS = 8
 HEAD_DIM = 64
 CAP = 48
+DP = "dp"
+FSDP = "fsdp"
 POOL_PLANES = 2
 POOL_SHARDS = 16
 PAD = 128
@@ -75,20 +77,21 @@
 
 
 def chip_masks():
-    return [2 * c for c in range(1, lax.axis_size("fsdp") // 2)]
+    return [2 * c for c in range(1, lax.axis_size(FSDP) // 2)]
 
 
 def gather_planes(rows, count):
     if count == 1:
         return rows
-    pieces = [rows] + [swap(rows, "dp", k) for k in range(1, count)]
+    step = lax.axis_size(DP) // count
+    pieces = [rows] + [swap(rows, DP, k * step) for k in range(1, count)]
     return jnp.concatenate(pieces, axis=0)
 
 
 def gather_pieces(rows, planes):
     first = gather_planes(rows, planes)
-    half = [first] + [swap(first, "fsdp", m) for m in chip_masks()]
-    return half + [swap(piece, "fsdp", 1) for piece in half]
+    half = [first] + [swap(first, FSDP, m) for m in chip_masks()]
+    return half + [swap(piece, FSDP, 1) for piece in half]
 
 
 def after(values, event):
@@ -96,30 +99,33 @@
 
 
 def scatter_chips(own_half, other_half, lead, event=None):
-    total = own_half.astype(f32) + swap(other_half.astype(bf16), "fsdp", 1).astype(f32)
+    total = own_half.astype(f32) + swap(other_half.astype(bf16), FSDP, 1).astype(
+        f32
+    )
     parts = total.astype(bf16)
     out = total[:lead]
     for c, m in enumerate(chip_masks(), 1):
-        piece = swap(parts[c * lead : (c + 1) * lead], "fsdp", m)
+        piece = swap(parts[c * lead : (c + 1) * lead], FSDP, m)
         piece = after(piece, event)
         out = out + piece.astype(f32)
     return out
 
 
 def scatter_all(own_half, other_half, rows, count, events=(None, None)):
+    step = lax.axis_size(DP) // count
     planes = scatter_chips(own_half, other_half, count * rows, events[0])
     parts = planes.astype(bf16)
     out = planes[:rows]
     for k in range(1, count):
-        piece = swap(parts[k * rows : (k + 1) * rows], "dp", k)
+        piece = swap(parts[k * rows : (k + 1) * rows], DP, k * step)
         out = out + after(piece, events[1]).astype(f32)
     return out
 
 
 def gather_rows(rows, planes):
     first = gather_planes(rows, planes)
-    half = jnp.concatenate([first] + [swap(first, "fsdp", m) for m in chip_masks()], axis=0)
-    return [half, swap(half, "fsdp", 1)]
+    half = jnp.concatenate([first] + [swap(first, FSDP, m) for m in chip_masks()], axis=0)
+    return [half, swap(half, FSDP, 1)]
 
 
 def expert_kernel(pieces, planes, held, tok_rows, width, ff, experts_total):
@@ -239,6 +245,244 @@
     )
 
 
+def mm(left, right, dims=((1,), (0,))):
+    return lax.dot_general(left, right, (dims, ((), ())), preferred_element_type=f32)
+
+
+def project_kernel(pieces, piece_rows, rows, width, gain_col, rotated, q_width):
+    def kernel(*refs):
+        tokens_ref, scale_ref, shuffle_ref, cos_ref, sin_ref = refs[:5]
+        piece_refs = refs[5 : 5 + pieces]
+        unit_ref, normed_ref, gain_ref, q_ref, kv_ref = refs[5 + pieces :]
+        unit = mm(tokens_ref[...], shuffle_ref[...]) * scale_ref[...]
+        unit_ref[...] = unit
+        projected = None
+        for i, piece_ref in enumerate(piece_refs):
+            at = slice(i * piece_rows, (i + 1) * piece_rows)
+            gain = piece_ref[:, gain_col:].astype(f32).T[:1, :]
+            gain_ref[:, at] = gain
+            normed = (unit[:, at] * gain).astype(bf16)
+            normed_ref[:, at] = normed
+            part = mm(normed, piece_ref[:, :gain_col])
+            projected = part if projected is None else projected + part
+        lane = lax.broadcasted_iota(jnp.int32, (rows, PAD), 1)
+        first_half = lane % HEAD_DIM < HEAD_DIM // 2
+        cos, sin = cos_ref[...], sin_ref[...]
+        for c in range(gain_col // PAD):
+            at = slice(c * PAD, (c + 1) * PAD)
+            x = projected[:, at]
+            if c * PAD < rotated:
+                other = jnp.where(
+                    first_half,
+                    -pltpu.roll(x, PAD - HEAD_DIM // 2, 1),
+                    pltpu.roll(x, HEAD_DIM // 2, 1),
+                )
+                x = x * cos + other * sin
+            if c * PAD < q_width:
+                q_ref[:, at] = x.astype(bf16)
+            else:
+                kv_ref[:, c * PAD - q_width : (c + 1) * PAD - q_width] = x.astype(bf16)
+
+    in_vmem = pl.BlockSpec(memory_space=pltpu.VMEM)
+    return pl.pallas_call(
+        kernel,
+        out_shape=[
+            jax.ShapeDtypeStruct((rows, width), f32),
+            jax.ShapeDtypeStruct((rows, width), bf16),
+            jax.ShapeDtypeStruct((1, width), f32),
+            jax.ShapeDtypeStruct((rows, q_width), bf16),
+            jax.ShapeDtypeStruct((rows, gain_col - q_width), bf16),
+        ],
+        in_specs=[in_vmem] * (5 + pieces),
+        out_specs=[in_vmem] * 5,
+        compiler_params=pltpu.CompilerParams(vmem_limit_bytes=40 * 1024 * 1024),
+        name="proj",
+    )
+
+
+def rotate_back(x, cos, sin):
+    lane = lax.broadcasted_iota(jnp.int32, x.shape, 1)
+    other = jnp.where(
+        lane % HEAD_DIM < HEAD_DIM // 2,
+        pltpu.roll(x, PAD - HEAD_DIM // 2, 1),
+        -pltpu.roll(x, HEAD_DIM // 2, 1),
+    )
+    return x * cos + other * sin
+
+
+def back_project_kernel(pieces, piece_rows, rows, width, q_width, kv_width):
+    gain_col = q_width + 2 * kv_width
+
+    def kernel(dq_ref, dkv_ref, cos_ref, sin_ref, *refs):
+        out_ref, dkv_out_ref = refs[pieces:]
+        cos, sin = cos_ref[...], sin_ref[...]
+        for c in range(kv_width // PAD):
+            at = slice(c * PAD, (c + 1) * PAD)
+            dkv_out_ref[:, at] = rotate_back(dkv_ref[:, at], cos, sin).astype(bf16)
+        dkv_out_ref[:, kv_width:] = dkv_ref[:, kv_width:].astype(bf16)
+        for i in range(pieces):
+            out_ref[:, i * piece_rows : (i + 1) * piece_rows] = mm(
+                dq_ref[...], refs[i][:, :q_width], ((1,), (1,))
+            ) + mm(dkv_out_ref[...], refs[i][:, q_width:gain_col], ((1,), (1,)))
+
+    in_vmem = pl.BlockSpec(memory_space=pltpu.VMEM)
+    return pl.pallas_call(
+        kernel,
+        out_shape=[
+            jax.ShapeDtypeStruct((rows, width), f32),
+            jax.ShapeDtypeStruct((rows, 2 * kv_width), bf16),
+        ],
+        in_specs=[in_vmem] * (4 + pieces),
+        out_specs=[in_vmem] * 2,
+        compiler_params=pltpu.CompilerParams(vmem_limit_bytes=40 * 1024 * 1024),
+        name="backproj",
+    )
+
+
+def attention_back_kernel(rows, keys, width, q_width, kv_width):
+    pair = q_width // kv_width
+    contract_last = ((1,), (1,))
+    half = keys // 2
+
+    def kernel(
+        dh_ref, own_ref, other_ref, shuffle_ref, att_ref, q_ref, kv_ref, lse_ref,
+        key_pos_ref, q_pos_ref, start_ref, cos_ref, sin_ref, dq_ref, dkv_own_ref, dkv_other_ref,
+    ):
+        dh = dh_ref[...]
+        do_rel = jnp.concatenate(
+            [mm(dh, ref[:, :width], contract_last) for ref in (own_ref, other_ref)], axis=1
+        ).astype(bf16)
+        d_att = mm(do_rel, shuffle_ref[...], contract_last).astype(bf16)
+        prod = (d_att.astype(f32) * att_ref[...].astype(f32)).T
+        allowed = (key_pos_ref[...] <= q_pos_ref[...]) & (key_pos_ref[...] >= start_ref[...])
+        cos, sin = cos_ref[...], sin_ref[...]
+
+        def stacked(x):
+            return jnp.concatenate(
+                [x[:, r * HEAD_DIM : (r + 1) * HEAD_DIM] for r in range(pair)], axis=0
+            )
+
+        def one_head(g):
+            at = slice(g * pair * HEAD_DIM, (g + 1) * pair * HEAD_DIM)
+            q = stacked(q_ref[:, at])
+            d_out = stacked(d_att[:, at])
+            key = kv_ref[:, g * HEAD_DIM : (g + 1) * HEAD_DIM]
+            val = kv_ref[:, kv_width + g * HEAD_DIM : kv_width + (g + 1) * HEAD_DIM]
+            delta = jnp.concatenate(
+                [
+                    jnp.sum(
+                        prod[(g * pair + r) * HEAD_DIM : (g * pair + r + 1) * HEAD_DIM],
+                        axis=0,
+                        keepdims=True,
+                    )
+                    for r in range(pair)
+                ],
+                axis=1,
+            )
+            scores = mm(key, q, contract_last) * score_scale
+            probs = jnp.where(allowed, jnp.exp(scores - lse_ref[g : g + 1, :]), 0.0)
+            d_probs = mm(val, d_out, contract_last)
+            d_scores = (probs * (d_probs - delta) * score_scale).astype(bf16)
+            dq = mm(d_scores, key, ((0,), (0,)))
+            dq = jnp.concatenate([dq[r * rows : (r + 1) * rows] for r in range(pair)], axis=1)
+            for c in range(pair * HEAD_DIM // PAD):
+                lanes = slice(c * PAD, (c + 1) * PAD)
+                dq_ref[:, at.start + c * PAD : at.start + (c + 1) * PAD] = rotate_back(
+                    dq[:, lanes], cos, sin
+                ).astype(bf16)
+            return mm(d_scores, q), mm(probs.astype(bf16), d_out)
+
+        per_store = PAD // HEAD_DIM
+        for c in range(kv_width // PAD):
+            heads = [one_head(c * per_store + i) for i in range(per_store)]
+            for j in range(2):
+                both = jnp.concatenate([h[j] for h in heads], axis=1)
+                lanes = slice(j * kv_width + c * PAD, j * kv_width + (c + 1) * PAD)
+                dkv_own_ref[:, lanes] = both[:half]
+                dkv_other_ref[:, lanes] = both[half:].astype(bf16)
+
+    in_vmem = pl.BlockSpec(memory_space=pltpu.VMEM)
+    return pl.pallas_call(
+        kernel,
+        out_shape=[
+            jax.ShapeDtypeStruct((rows, q_width), bf16),
+            jax.ShapeDtypeStruct((half, 2 * kv_width), f32),
+            jax.ShapeDtypeStruct((half, 2 * kv_width), bf16),
+        ],
+        in_specs=[in_vmem] * 13,
+        out_specs=[in_vmem] * 3,
+        compiler_params=pltpu.CompilerParams(vmem_limit_bytes=56 * 1024 * 1024),
+        name="attback",
+    )
+
+
+def attention_kernel(rows, keys, width, q_width, kv_width):
+    pair = q_width // kv_width
+    contract_last = ((1,), (1,))
+    half = keys // 2
+
+    def kernel(
+        q_ref, first_ref, second_ref, key_pos_ref, q_pos_ref, start_ref, shuffle_ref, own_ref,
+        other_ref, tokens_ref, gain_ref, att_ref, rel_ref, hidden_ref, unit_ref, normed_ref,
+        scale_ref, lse_ref, kv_ref,
+    ):
+        kv_ref[:half] = first_ref[...]
+        kv_ref[half:] = second_ref[...]
+        allowed = (key_pos_ref[...] <= q_pos_ref[...]) & (key_pos_ref[...] >= start_ref[...])
+
+        def one_head(g):
+            at = g * pair * HEAD_DIM
+            q = jnp.concatenate(
+                [q_ref[:, at + r * HEAD_DIM : at + (r + 1) * HEAD_DIM] for r in range(pair)], axis=0
+            )
+            key = kv_ref[:, g * HEAD_DIM : (g + 1) * HEAD_DIM]
+            val = kv_ref[:, kv_width + g * HEAD_DIM : kv_width + (g + 1) * HEAD_DIM]
+            scores = jnp.where(allowed, mm(key, q, contract_last) * score_scale, masked_low)
+            top = jnp.max(scores, axis=0, keepdims=True)
+            raised = jnp.where(allowed, jnp.exp(scores - top), 0.0)
+            total = jnp.sum(raised, axis=0, keepdims=True)
+            lse_ref[g : g + 1, :] = top + jnp.log(total)
+            probs = (raised / total).astype(bf16)
+            out = mm(probs, val, ((0,), (0,)))
+            att_ref[:, at : at + pair * HEAD_DIM] = jnp.concatenate(
+                [out[r * rows : (r + 1) * rows] for r in range(pair)], axis=1
+            ).astype(bf16)
+
+        for g in range(kv_width // HEAD_DIM):
+            one_head(g)
+        rel = mm(att_ref[...], shuffle_ref[...]).astype(bf16)
+        rel_ref[...] = rel
+        hidden = tokens_ref[...].astype(f32) + (
+            mm(rel[:, : width // 2], own_ref[:, :width])
+            + mm(rel[:, width // 2 :], other_ref[:, :width])
+        )
+        hidden_ref[...] = hidden
+        scale = lax.rsqrt(jnp.mean(hidden * hidden, axis=1, keepdims=True) + norm_eps)
+        scale_ref[...] = scale
+        unit = hidden * scale
+        unit_ref[...] = unit
+        normed_ref[...] = (unit * gain_ref[...]).astype(bf16)
+
+    in_vmem = pl.BlockSpec(memory_space=pltpu.VMEM)
+    return pl.pallas_call(
+        kernel,
+        out_shape=[
+            jax.ShapeDtypeStruct((rows, q_width), bf16),
+            jax.ShapeDtypeStruct((rows, q_width), bf16),
+            jax.ShapeDtypeStruct((rows, width), f32),
+            jax.ShapeDtypeStruct((rows, width), f32),
+            jax.ShapeDtypeStruct((rows, width), bf16),
+            jax.ShapeDtypeStruct((rows, 1), f32),
+            jax.ShapeDtypeStruct((kv_width // HEAD_DIM, pair * rows), f32),
+            jax.ShapeDtypeStruct((keys, 2 * kv_width), bf16),
+        ],
+        in_specs=[in_vmem] * 11,
+        out_specs=[in_vmem] * 8,
+        compiler_params=pltpu.CompilerParams(vmem_limit_bytes=56 * 1024 * 1024),
+        name="wo",
+    )
+
+
 def local(
     tokens,
     seq_starts,
@@ -254,10 +498,10 @@
     expert_out,
     d_out,
 ):
-    fsdp_count = lax.axis_size("fsdp")
-    dp_count = lax.axis_size("dp")
-    fsdp_at = lax.axis_index("fsdp")
-    dp_at = lax.axis_index("dp")
+    fsdp_count = lax.axis_size(FSDP)
+    dp_count = lax.axis_size(DP)
+    fsdp_at = lax.axis_index(FSDP)
+    dp_at = lax.axis_index(DP)
     chips = fsdp_count // 2
     tok_rows, width = tokens.shape
     own_rows = w_query.shape[0]
@@ -313,16 +557,22 @@
     )
     d_pool = gather_pieces(d_pack, planes)
 
-    group_at = dp_at % planes
+    top = dp_count // planes
+    group_at = dp_at // top
+    low_bits = [1 << i for i in range(top.bit_length() - 1)]
     in_groups = expert_in.reshape(planes, held, slice_width, ff_two)
     out_groups = expert_out.reshape(planes, held, ff, slice_width)
-    in_parts, out_parts = [], []
-    for k in range(dp_count):
-        target = group_at ^ (k % planes)
-        in_piece = lax.dynamic_index_in_dim(in_groups, target, 0, keepdims=False)
-        out_piece = lax.dynamic_index_in_dim(out_groups, target, 0, keepdims=False)
-        in_parts.append(in_piece if k == 0 else swap(in_piece, "dp", k))
-        out_parts.append(out_piece if k == 0 else swap(out_piece, "dp", k))
+    in_parts, out_parts = {}, {}
+    for groups, parts in ((in_groups, in_parts), (out_groups, out_parts)):
+        parts[0] = lax.dynamic_index_in_dim(groups, group_at, 0, keepdims=False)
+        for j in range(1, planes):
+            away = lax.dynamic_index_in_dim(groups, group_at ^ j, 0, keepdims=False)
+            parts[j * top] = swap(away, DP, j * top)
+        for bit in low_bits:
+            for k in sorted(parts):
+                parts[k | bit] = swap(parts[k], DP, bit)
+    out_parts = [out_parts[k] for k in range(dp_count)]
+
     token_index = jnp.arange(tok_rows, dtype=jnp.int32)
     global_pos = fsdp_at * tok_rows + token_index
     second_start = seq_starts[0, 1]
@@ -330,53 +580,71 @@
     cosine_table, sine_values = rope_tables(global_pos - sequence_start, HEAD_DIM)
     tok_f32 = tokens.astype(f32)
     scale_one = lax.rsqrt(jnp.mean(tok_f32 * tok_f32, axis=-1, keepdims=True) + norm_eps)
-    unit_one = dot(tokens, shuffle, ((1,), (0,))) * scale_one
     gain_col = q_width + 2 * kv_width
-    gain_one = jnp.concatenate([piece[:, gain_col] for piece in qkv_pieces]).astype(f32)[None, :]
-    first_normed = (unit_one * gain_one).astype(bf16)
-    projected = sum(
-        dot(first_normed[:, i * piece.shape[0] : (i + 1) * piece.shape[0]], piece, ((1,), (0,)))
-        for i, piece in enumerate(qkv_pieces)
-    )
-    query_rows = apply_rotation(
-        projected[:, :q_width].reshape(tok_rows, QUERY_HEADS, HEAD_DIM), cosine_table, sine_values
-    ).astype(bf16)
-    key_rows = apply_rotation(
-        projected[:, q_width : q_width + kv_width].reshape(tok_rows, KEY_HEADS, HEAD_DIM),
-        cosine_table,
-        sine_values,
-    ).astype(bf16)
-    value_rows = projected[:, q_width + kv_width : q_width + 2 * kv_width].astype(bf16)
-    kv_rows = jnp.concatenate([key_rows.reshape(tok_rows, kv_width), value_rows], axis=1)
-    kv_all = jnp.concatenate(gather_rows(kv_rows, 1), axis=0)
+    piece_rows = qkv_pieces[0].shape[0]
+    wide = (1, 2 * PAD // HEAD_DIM)
+    cos_wide, sin_wide = jnp.tile(cosine_table, wide), jnp.tile(sine_values, wide)
+    if piece_rows % PAD == 0:
+        run = project_kernel(
+            len(qkv_pieces), piece_rows, tok_rows, width, gain_col, q_width + kv_width, q_width
+        )
+        wide = (1, 2 * PAD // HEAD_DIM)
+        unit_one, first_normed, gain_one, query_rows, kv_rows = run(
+            tokens,
+            scale_one,
+            shuffle,
+            cos_wide,
+            sin_wide,
+            *qkv_pieces,
+        )
+    else:
+        unit_one = dot(tokens, shuffle, ((1,), (0,))) * scale_one
+        gain_one = jnp.concatenate([piece[:, gain_col] for piece in qkv_pieces]).astype(f32)[None, :]
+        first_normed = (unit_one * gain_one).astype(bf16)
+        projected = sum(
+            dot(first_normed[:, i * piece.shape[0] : (i + 1) * piece.shape[0]], piece, ((1,), (0,)))
+            for i, piece in enumerate(qkv_pieces)
+        )
+        query_rows = apply_rotation(
+            projected[:, :q_width].reshape(tok_rows, QUERY_HEADS, HEAD_DIM), cosine_table, sine_values
+        ).astype(bf16)
+        key_rows = apply_rotation(
+            projected[:, q_width : q_width + kv_width].reshape(tok_rows, KEY_HEADS, HEAD_DIM),
+            cosine_table,
+            sine_values,
+        ).astype(bf16)
+        value_rows = projected[:, q_width + kv_width : q_width + 2 * kv_width].astype(bf16)
+        kv_rows = jnp.concatenate([key_rows.reshape(tok_rows, kv_width), value_rows], axis=1)
+    kv_first, kv_second = gather_rows(kv_rows, 1)
     shard = jnp.arange(fsdp_count, dtype=jnp.int32)
     shard_dev = (2 * (shard % chips) + shard // chips) ^ fsdp_at
     key_pos = (shard_dev[:, None] * tok_rows + token_index[None, :]).reshape(-1)
-    allowed = (key_pos[None, :] <= global_pos[:, None]) & (
-        key_pos[None, :] >= sequence_start[:, None]
-    )
-    keys = kv_all[:, :kv_width].reshape(-1, KEY_HEADS, HEAD_DIM)
-    vals = kv_all[:, kv_width:].reshape(-1, KEY_HEADS, HEAD_DIM)
-    grouped = query_rows.reshape(tok_rows, KEY_HEADS, heads_per_key, HEAD_DIM)
-    mask = allowed[None, None]
-    scores = (
-        jnp.einsum("tgrd,kgd->grtk", grouped, keys, preferred_element_type=f32) * score_scale
-    )
-    row_max = jnp.max(jnp.where(mask, scores, masked_low), axis=-1, keepdims=True)
-    summed = jnp.sum(jnp.where(mask, jnp.exp(scores - row_max), 0.0), axis=-1, keepdims=True)
-    lse = row_max + jnp.log(summed)
-    probs = jnp.where(mask, jnp.exp(scores - lse), 0.0)
-    probs_b = probs.astype(bf16)
-    attended = jnp.einsum("grtk,kgd->tgrd", probs_b, vals, preferred_element_type=f32).astype(bf16)
-    attended_rows = attended.reshape(tok_rows, q_width)
-    attended_rel = dot(attended_rows, shuffle, ((1,), (0,))).astype(bf16)
-    hidden = tok_f32 + (
-        dot(attended_rel[:, :half_width], output_own[:, :width], ((1,), (0,)))
-        + dot(attended_rel[:, half_width:], output_other[:, :width], ((1,), (0,)))
-    )
-    scale_two = lax.rsqrt(jnp.mean(hidden * hidden, axis=-1, keepdims=True) + norm_eps)
-    unit_two = hidden * scale_two
-    normed_two = (unit_two * gain_two).astype(bf16)
+    pair = (1, heads_per_key)
+    key_column = key_pos[:, None]
+    q_row, start_row = jnp.tile(global_pos[None], pair), jnp.tile(sequence_start[None], pair)
+    run = attention_kernel(tok_rows, key_pos.shape[0], width, q_width, kv_width)
+    (
+        attended_rows,
+        attended_rel,
+        hidden,
+        unit_two,
+        normed_two,
+        scale_two,
+        lse,
+        kv_all,
+    ) = run(
+        query_rows.reshape(tok_rows, q_width),
+        kv_first,
+        kv_second,
+        key_column,
+        q_row,
+        start_row,
+        shuffle,
+        output_own,
+        output_other,
+        tokens,
+        gain_two,
+    )
 
     normed_pool = gather_pieces(normed_two, planes)
     win = jnp.zeros((held, width, ff_two), bf16)
@@ -415,15 +683,26 @@
     )
     back = scatter_all(back_own, back_other, tok_rows, planes)
 
-    in_sent, out_sent = [], []
-    for k in range(dp_count):
-        target = dp_at ^ k
-        in_piece = lax.dynamic_slice_in_dim(grad_in_b, target * slice_width, slice_width, 1)
-        out_piece = lax.dynamic_slice_in_dim(grad_out_b, target * slice_width, slice_width, 2)
-        if k:
-            in_piece, out_piece = swap(in_piece, "dp", k), swap(out_piece, "dp", k)
-        in_sent.append(in_piece)
-        out_sent.append(out_piece)
+    in_sent, out_sent, in_near, out_near = [], [], [], []
+    for grads, axis, sent, near in (
+        (grad_in_b, 1, in_sent, in_near), (grad_out_b, 2, out_sent, out_near)
+    ):
+        left = {
+            k: lax.dynamic_slice_in_dim(grads, (dp_at ^ k) * slice_width, slice_width, axis)
+            for k in range(dp_count)
+        }
+        for bit in reversed(low_bits):
+            for k in sorted(left, reverse=True):
+                if k & bit:
+                    moved = swap(left.pop(k), DP, bit)
+                    if k == bit:
+                        near.append(moved)
+                        continue
+                    kept = left[k ^ bit].astype(f32) + moved.astype(f32)
+                    left[k ^ bit] = kept.astype(bf16) if k >= top else kept
+        sent.append(left[0])
+        for j in range(1, planes):
+            sent.append(swap(left[j * top].astype(bf16), DP, j * top))
 
     d_block = d_out.astype(f32)
     d_gate = (
@@ -437,48 +716,46 @@
     d_hidden = d_block + d_hidden_two
     d_hidden_b = d_hidden.astype(bf16)
     normed_two_rel = dot(normed_two, shuffle, ((1,), (0,))).astype(bf16)
-    gain_two_rel = jnp.dot(
-        grad_gain_two[None, :], shuffle.astype(f32), precision=lax.Precision.HIGHEST
-    )[0]
+    gain_two_high = grad_gain_two.astype(bf16)
+    gain_two_low = (grad_gain_two - gain_two_high.astype(f32)).astype(bf16)
+    gain_two_rel = jnp.sum(
+        dot(jnp.stack([gain_two_high, gain_two_low]), shuffle, ((1,), (0,))), axis=0
+    )
     grad_output_own = dot(attended_rel[:, :half_width], d_hidden_b, ((0,), (0,)))
     grad_output_other = dot(attended_rel[:, half_width:], d_hidden_b, ((0,), (0,))).astype(bf16)
     grad_router_rel = dot(normed_two_rel, d_logits, ((0,), (0,)))
 
-    grad_attended_rel = jnp.concatenate(
-        [
-            dot(d_hidden_b, output_own[:, :width], ((1,), (1,))),
-            dot(d_hidden_b, output_other[:, :width], ((1,), (1,))),
-        ],
-        axis=1,
-    ).astype(bf16)
-    grad_attended = dot(grad_attended_rel, shuffle, ((1,), (1,))).astype(bf16)
-    grad_grouped = grad_attended.reshape(tok_rows, KEY_HEADS, heads_per_key, HEAD_DIM)
-    delta = jnp.sum(grad_grouped.astype(f32) * attended.astype(f32), axis=-1).transpose(1, 2, 0)
-    d_vals = jnp.einsum("grtk,tgrd->kgd", probs_b, grad_grouped, preferred_element_type=f32)
-    d_probs = jnp.einsum("tgrd,kgd->grtk", grad_grouped, vals, preferred_element_type=f32)
-    d_scores = (probs * (d_probs - delta[..., None]) * score_scale).astype(bf16)
-    d_queries = jnp.einsum("grtk,kgd->tgrd", d_scores, keys, preferred_element_type=f32)
-    d_keys = jnp.einsum("grtk,tgrd->kgd", d_scores, grouped, preferred_element_type=f32)
-    d_kv = jnp.concatenate([d_keys.reshape(-1, kv_width), d_vals.reshape(-1, kv_width)], axis=1)
-    split_at = chips * tok_rows
-    d_kv_own = scatter_chips(d_kv[:split_at], d_kv[split_at:].astype(bf16), tok_rows)
+    run = attention_back_kernel(tok_rows, key_pos.shape[0], width, q_width, kv_width)
+    d_query_b, d_kv_first, d_kv_second = run(
+        d_hidden_b,
+        output_own,
+        output_other,
+        shuffle,
+        attended_rows,
+        query_rows.reshape(tok_rows, q_width),
+        kv_all,
+        lse,
+        key_column,
+        q_row,
+        start_row,
+        cos_wide,
+        sin_wide,
+    )
+    d_kv_own = scatter_chips(d_kv_first, d_kv_second, tok_rows)
     summed_output = scatter_all(grad_output_own, grad_output_other, own_rows, dp_count)
-    d_query_b = apply_rotation(
-        d_queries.reshape(tok_rows, QUERY_HEADS, HEAD_DIM), cosine_table, -sine_values
-    ).astype(bf16)
-    d_key_b = apply_rotation(
-        d_kv_own[:, :kv_width].reshape(tok_rows, KEY_HEADS, HEAD_DIM), cosine_table, -sine_values
-    ).astype(bf16)
-    d_proj = jnp.concatenate(
-        [
-            d_query_b.reshape(tok_rows, q_width),
-            d_key_b.reshape(tok_rows, kv_width),
-            d_kv_own[:, kv_width:].astype(bf16),
-        ],
-        axis=1,
-    )
-    qkv_all = jnp.concatenate(qkv_pieces, axis=0)
-    d_normed_one = dot(d_proj, qkv_all[:, :gain_col], ((1,), (1,)))
+    if piece_rows % PAD == 0:
+        run = back_project_kernel(
+            len(qkv_pieces), piece_rows, tok_rows, width, q_width, kv_width
+        )
+        d_normed_one, d_kv_b = run(d_query_b, d_kv_own, cos_wide, sin_wide, *qkv_pieces)
+    else:
+        d_key_b = apply_rotation(
+            d_kv_own[:, :kv_width].reshape(tok_rows, KEY_HEADS, HEAD_DIM), cosine_table, -sine_values
+        ).reshape(tok_rows, kv_width)
+        d_kv_b = jnp.concatenate([d_key_b, d_kv_own[:, kv_width:]], axis=1).astype(bf16)
+        d_proj = jnp.concatenate([d_query_b, d_kv_b], axis=1)
+        qkv_all = jnp.concatenate(qkv_pieces, axis=0)
+        d_normed_one = dot(d_proj, qkv_all[:, :gain_col], ((1,), (1,)))
     d_tok_rel, grad_gain_one = norm_backward(d_normed_one, unit_one, scale_one, gain_one)
     high = d_tok_rel.astype(bf16)
     low = (d_tok_rel - high.astype(f32)).astype(bf16)
@@ -492,33 +769,42 @@
         ],
         axis=1,
     )
-    summed_qkv = scatter_all(
-        dot(first_normed[:, :half_width], d_proj, ((0,), (0,))),
-        dot(first_normed[:, half_width:], d_proj, ((0,), (0,))).astype(bf16),
-        own_rows,
-        dp_count,
-    )
+    normed_own, normed_other = first_normed[:, :half_width], first_normed[:, half_width:]
+    summed_q, summed_kv = [
+        scatter_all(
+            dot(normed_own, d_rows, ((0,), (0,))),
+            dot(normed_other, d_rows, ((0,), (0,))).astype(bf16),
+            own_rows,
+            dp_count,
+        )
+        for d_rows in (d_query_b, d_kv_b)
+    ]
     summed_small = scatter_all(grad_small[:half_width], grad_small[half_width:], own_rows, dp_count)
 
-    mixture = scatter_all(mix_own, mix_other, tok_rows, planes, (grad_attended, d_proj))
+    mixture = scatter_all(mix_own, mix_other, tok_rows, planes, (d_query_b, d_kv_b))
     block_out = (hidden + mixture).astype(bf16)
 
-    in_sent, out_sent = after((in_sent, out_sent), d_proj)
-    in_back, out_back = [None] * planes, [None] * planes
-    for k in range(dp_count):
-        j = k % planes
-        for back_list, sent in ((in_back, in_sent), (out_back, out_sent)):
-            piece = sent[k].astype(f32)
-            back_list[j] = piece if back_list[j] is None else back_list[j] + piece
-    d_expert_in = jnp.concatenate(ordered(in_back, group_at), axis=0)
-    d_expert_out = jnp.concatenate(ordered(out_back, group_at), axis=0)
+    in_sent, out_sent, in_near, out_near = after((in_sent, out_sent, in_near, out_near), d_kv_b)
+    in_back = [piece.astype(f32) for piece in in_sent]
+    out_back = [piece.astype(f32) for piece in out_sent]
+    in_back[0] = sum((piece.astype(f32) for piece in in_near), in_back[0])
+    out_back[0] = sum((piece.astype(f32) for piece in out_near), out_back[0])
+    group_axis = jnp.arange(planes, dtype=jnp.int32)[:, None, None, None] ^ group_at
+    totals = []
+    for back_list in (in_back, out_back):
+        total = back_list[0][None]
+        for j in range(1, planes):
+            total = jnp.where(group_axis == j, back_list[j][None], total)
+        total = jnp.broadcast_to(total, (planes,) + back_list[0].shape)
+        totals.append(total.reshape((local_experts,) + back_list[0].shape[1:]))
+    d_expert_in, d_expert_out = totals
     return (
         block_out,
         d_tokens,
         summed_small[:, experts_total],
-        summed_qkv[:, :q_width],
-        summed_qkv[:, q_width : q_width + kv_width],
-        summed_qkv[:, q_width + kv_width : gain_col],
+        summed_q,
+        summed_kv[:, :kv_width],
+        summed_kv[:, kv_width:],
         summed_output,
         summed_small[:, experts_total + 1],
         summed_small[:, :experts_total],
@@ -529,31 +815,31 @@
 
 def solution(mesh):
     in_specs = (
-        P(("dp", "fsdp"), None),
-        P("dp", None),
-        P(("dp", "fsdp"), None),
-        P(("dp", "fsdp")),
-        P(("dp", "fsdp"), None),
-        P(("dp", "fsdp"), None),
-        P(("dp", "fsdp"), None),
-        P(("dp", "fsdp"), None),
-        P(("dp", "fsdp")),
-        P(("dp", "fsdp"), None),
-        P("fsdp", "dp", None),
-        P("fsdp", None, "dp"),
-        P(("dp", "fsdp"), None),
+        P((DP, FSDP), None),
+        P(DP, None),
+        P((DP, FSDP), None),
+        P((DP, FSDP)),
+        P((DP, FSDP), None),
+        P((DP, FSDP), None),
+        P((DP, FSDP), None),
+        P((DP, FSDP), None),
+        P((DP, FSDP)),
+        P((DP, FSDP), None),
+        P(FSDP, DP, None),
+        P(FSDP, None, DP),
+        P((DP, FSDP), None),
     )
     out_specs = (
-        P(("dp", "fsdp"), None),
-        P(("dp", "fsdp"), None),
-        P(("dp", "fsdp")),
-        P(("dp", "fsdp"), None),
-        P(("dp", "fsdp"), None),
-        P(("dp", "fsdp"), None),
-        P(("dp", "fsdp"), None),
-        P(("dp", "fsdp")),
-        P(("dp", "fsdp"), None),
-        P("fsdp", "dp", None),
-        P("fsdp", None, "dp"),
+        P((DP, FSDP), None),
+        P((DP, FSDP), None),
+        P((DP, FSDP)),
+        P((DP, FSDP), None),
+        P((DP, FSDP), None),
+        P((DP, FSDP), None),
+        P((DP, FSDP), None),
+        P((DP, FSDP)),
+        P((DP, FSDP), None),
+        P(FSDP, DP, None),
+        P(FSDP, None, DP),
     )
     return jax.shard_map(local, mesh=mesh, in_specs=in_specs, out_specs=out_specs, check_vma=False)

time: 647 us -> 547 us (0.85)
  waiting for transfers between devices: 300 us -> 228 us
  matrix products: 52 us -> 19.2 us
  Pallas kernels: 30.8 us -> 62.9 us
  starting transfers between devices: 124 us -> 102 us
  local copies, waits for them, and re-layouts: 80.8 us -> 70.7 us
    ppermute x84 -> x91, waiting for transfers between devices: 300 us -> 228 us  [swap(): return lax.ppermute(values, axis, [(i, i ^ mask) for i in range(count)])]
    pallas_call x0 -> x4, Pallas kernels: none -> 32.5 us  [the longest x1 14.3 us: local(): run(d_hidden_b, output_own, output_other, shuffle, attended_rows, query_r...]
    ppermute x84 -> x91, starting transfers between devices: 124 us -> 102 us  [swap(): return lax.ppermute(values, axis, [(i, i ^ mask) for i in range(count)])]
    dot_general x7 -> x0, matrix products: 18.9 us -> none  [the longest x1 5.17 us: local(): jnp.einsum('grtk,tgrd->kgd', probs_b, grad_grouped, preferred_element_typ...]
    dot_general x27 -> x14, matrix products: 32.9 us -> 19.1 us  [dot(): lax.dot_general(left, right, (dims, ((), ())), preferred_element_type=f32)]
    unnamed x219 -> x153, local copies, waits for them, and re-layouts: 27.2 us -> 17.8 us
    slice x31 -> x14, local copies, waits for them, and re-layouts: 12.8 us -> 4.52 us  [the longest x6 2.52 us: scatter_all(): piece = swap(parts[k * rows:(k + 1) * rows], DP, k * step)]
    concatenate x7 -> x0, other arithmetic: 7.03 us -> none  [the longest x1 2.77 us: local(): d_expert_in = jnp.concatenate(ordered(in_back, group_at), axis=0)]
  transfers between devices with their start and end apart: 84 -> 91, of which waited for: 26 -> 26; matrix products, arithmetic and copies ran while one was open for 27% -> 25% of each run, Pallas kernels for 0% -> 6%
where the time goes in v2:
time: 547 us; the launch traced here: 537 us
  waiting for transfers between devices  228 us (42%)
  starting transfers between devices  102 us (19%)
  local copies, waits for them, and re-layouts  70.7 us (13%)
  Pallas kernels  62.9 us (11%)
  other arithmetic  51.4 us (9%)
  matrix products  19.2 us (4%)
    ppermute x91, waiting for transfers between devices, swap(): return lax.ppermute(values, axis, [(i, i ^ mask) for i in range(count)])  228 us
    ppermute x91, starting transfers between devices, swap(): return lax.ppermute(values, axis, [(i, i ^ mask) for i in range(count)])  102 us
    pallas_call x1, Pallas kernels, local(): run(first_expert[None], router_w.T, chosen_rows, slots, win, wout, *norme...  30.4 us
    dot_general x14, matrix products, dot(): lax.dot_general(left, right, (dims, ((), ())), preferred_element_type=f32)  19.1 us
    unnamed x153, local copies, waits for them, and re-layouts  17.8 us
    pallas_call x1, Pallas kernels, local(): run(d_hidden_b, output_own, output_other, shuffle, attended_rows, query_r...  14.3 us
    another operation x16, local copies, waits for them, and re-layouts, local(): jnp.stack([x[:, width:width + expert_ids.shape[1]] for x in d_pool])  11.9 us
    pallas_call x1, Pallas kernels, local(): run(query_rows.reshape(tok_rows, q_width), kv_first, kv_second, key_colum...  11.4 us
  transfers between devices with their start and end apart: 91, of which 26 were waited for; matrix products, arithmetic and copies ran while one was open for 25% of the time, Pallas kernels for 6%

profile of v2, /device:TPU:0, one launch (start us, length us, event | category | flops | bytes accessed | tf_op | source)
XLA Modules:
  0.0 536.6 jit_solution(6942480544045101308)
XLA Ops:
  3.0 3.1 collective-permute-start
  6.1 2.6 collective-permute-start.1
  11.9 3.5 collective-permute-start.15
  30.9 2.5 broadcast_in_dim.141
  38.7 4.2 collective-permute-done.16
  43.0 9.7 %collective-permute-start.34 = (bf16[2,512,256]{2,1,0:T(8,128)(2,1)}, bf16[2,512,256]{2,1,0:T(8,128)(2,1)}, u32[]{:S(2)}, u32[]{:S(2)}) collective-permute-start(bf16[2,512,256]{2,1,0:T(8,128)(2,1)} %get-tuple-element.133), channel_id=1, source_target_pairs={{0,8},{8,0},{16,24},{24,16},{1,9},{9,1},{17,25},{25,17},{2,10},{10... | collective-permute-start | bytes 1572872 | tf_op jit(solution)/shard_map/ppermute | solution.py:33
  60.8 15.5 %collective-permute-done.21 = bf16[128,1152]{1,0:T(8,128)(2,1)S(1)} collective-permute-done((bf16[128,1152]{1,0:T(8,128)(2,1)S(1)}, bf16[128,1152]{1,0:T(8,128)(2,1)S(1)}, u32[]{:S(2)}, u32[]{:S(2)}) %collective-permute-start.21) | collective-permute-done | bytes 294944 | tf_op jit(solution)/shard_map/ppermute | solution.py:33
  87.4 2.4 collective-permute-start.24
  91.5 8.5 %collective-permute-done.22.refs_15_ = bf16[256,1152]{1,0:T(8,128)(2,1)S(1)} collective-permute-done((bf16[256,1152]{1,0:T(8,128)(2,1)}, bf16[256,1152]{1,0:T(8,128)(2,1)S(1)}, u32[]{:S(2)}, u32[]{:S(2)}) %collective-permute-start.22) | collective-permute-done | bytes 589856 | tf_op jit(solution)/shard_map/ppermute | solution.py:33
  102.4 8.9 %collective-permute-done.23.refs_16_ = bf16[256,1152]{1,0:T(8,128)(2,1)} collective-permute-done((bf16[256,1152]{1,0:T(8,128)(2,1)}, bf16[256,1152]{1,0:T(8,128)(2,1)}, u32[]{:S(2)}, u32[]{:S(2)}) %collective-permute-start.23) | collective-permute-done | bytes 589856 | tf_op jit(solution)/shard_map/ppermute | solution.py:33
  114.2 2.5 collective-permute-start.5
  118.7 5.9 %collective-permute-done.3.refs_6_.refs_1_ = bf16[128,2176]{1,0:T(8,128)(2,1)S(1)} collective-permute-done((bf16[128,2176]{1,0:T(8,128)(2,1)S(1)}, bf16[128,2176]{1,0:T(8,128)(2,1)S(1)}, u32[]{:S(2)}, u32[]{:S(2)}) %collective-permute-start.3) | collective-permute-done | bytes 557088 | tf_op jit(solution)/shard_map/ppermute | solution.py:33
  124.6 10.9 %collective-permute-done.4.refs_7_.refs_2_ = bf16[128,2176]{1,0:T(8,128)(2,1)} collective-permute-done((bf16[128,2176]{1,0:T(8,128)(2,1)S(1)}, bf16[128,2176]{1,0:T(8,128)(2,1)}, u32[]{:S(2)}, u32[]{:S(2)}) %collective-permute-start.4) | collective-permute-done | bytes 557088 | tf_op jit(solution)/shard_map/ppermute | solution.py:33
  141.9 16.3 %collective-permute-done.33 = bf16[2,512,256]{2,1,0:T(8,128)(2,1)} collective-permute-done((bf16[2,512,256]{2,1,0:T(8,128)(2,1)}, bf16[2,512,256]{2,1,0:T(8,128)(2,1)}, u32[]{:S(2)}, u32[]{:S(2)}) %collective-permute-start.33) | collective-permute-done | bytes 524320 | tf_op jit(solution)/shard_map/ppermute | solution.py:33
  161.9 3.6 proj.1
  175.3 7.1 %collective-permute-done.11 = bf16[128,1024]{1,0:T(8,128)(2,1)S(1)} collective-permute-done((bf16[128,1024]{1,0:T(8,128)(2,1)S(1)}, bf16[128,1024]{1,0:T(8,128)(2,1)S(1)}, u32[]{:S(2)}, u32[]{:S(2)}) %collective-permute-start.11) | collective-permute-done | bytes 262176 | tf_op jit(solution)/shard_map/ppermute | solution.py:33
  183.1 20.3 %collective-permute-done.30 = bf16[2,256,1024]{2,1,0:T(8,128)(2,1)} collective-permute-done((bf16[2,256,1024]{2,1,0:T(8,128)(2,1)}, bf16[2,256,1024]{2,1,0:T(8,128)(2,1)}, u32[]{:S(2)}, u32[]{:S(2)}) %collective-permute-start.30) | collective-permute-done | bytes 1048608 | tf_op jit(solution)/shard_map/ppermute | solution.py:33
  211.0 11.4 %wo.1 = (bf16[128,1024]{1,0:T(8,128)(2,1)}, bf16[128,1024]{1,0:T(8,128)(2,1)}, f32[128,1024]{1,0:T(8,128)}, f32[128,1024]{1,0:T(8,128)}, bf16[128,1024]{1,0:T(8,...) custom-call(bf16[128,1024]{1,0:T(8,128)(2,1)} %copy-done.12, ...), custom_call_target="tpu_custom_call" | custom-call | tf_op jit(solution)/shard_map/wo/pallas_call | solution.py:635
  222.4 3.4 collective-permute-start.35
  227.5 8.0 %collective-permute-done.35 = bf16[128,1024]{1,0:T(8,128)(2,1)S(1)} collective-permute-done((bf16[128,1024]{1,0:T(8,128)(2,1)}, bf16[128,1024]{1,0:T(8,128)(2,1)S(1)}, u32[]{:S(2)}, u32[]{:S(2)}) %collective-permute-start.35) | collective-permute-done | bytes 262176 | tf_op jit(solution)/shard_map/ppermute | solution.py:33
  245.2 5.2 collective-permute-done.36.refs_7_
  250.5 11.1 %collective-permute-done.37.refs_8_ = bf16[256,1024]{1,0:T(8,128)(2,1)} collective-permute-done((bf16[256,1024]{1,0:T(8,128)(2,1)S(1)}, bf16[256,1024]{1,0:T(8,128)(2,1)}, u32[]{:S(2)}, u32[]{:S(2)}) %collective-permute-start.37) | collective-permute-done | bytes 524320 | tf_op jit(solution)/shard_map/ppermute | solution.py:33
  268.2 30.4 %experts.1 = (bf16[1024,1152]{1,0:T(8,128)(2,1)}, bf16[1024,1152]{1,0:T(8,128)(2,1)}, bf16[1024,1024]{1,0:T(8,128)(2,1)}, bf16[1024,1024]{1,0:T(8,128)(2,1)}, bf...) custom-call(s32[1]{0:T(128)} %bitcast.11.refs_0_, bf16[32,1024]{1,0:T(8,128)(2,1)} %slice_bitcast_fusion.7.refs_1_, ...), custom_call_target="tpu_custom_call" | custom-call | tf_op jit(solution)/shard_map/experts/pallas_call | solution.py:681
  300.2 2.5 constant_dynamic-slice_fusion
  302.8 4.3 collective-permute-start.87
  307.0 3.4 constant_dynamic-slice_fusion.1
  314.7 5.1 collective-permute-done.87
  323.2 18.9 %collective-permute-done.85 = bf16[2,256,1024]{2,1,0:T(8,128)(2,1)S(1)} collective-permute-done((bf16[2,256,1024]{2,1,0:T(8,128)(2,1)S(1)}, bf16[2,256,1024]{2,1,0:T(8,128)(2,1)S(1)}, u32[]{:S(2)}, u32[]{:S(2)}) %collective-permute-start.85) | collective-permute-done | bytes 1048608 | tf_op jit(solution)/shard_map/ppermute | solution.py:33
  342.1 2.6 add_convert_fusion
  346.7 3.1 fusion.107
  353.6 7.6 %collective-permute-done.49 = bf16[128,1152]{1,0:T(8,128)(2,1)S(1)} collective-permute-done((bf16[128,1152]{1,0:T(8,128)(2,1)S(1)}, bf16[128,1152]{1,0:T(8,128)(2,1)S(1)}, u32[]{:S(2)}, u32[]{:S(2)}) %collective-permute-start.49) | collective-permute-done | bytes 294944 | tf_op jit(solution)/shard_map/ppermute | solution.py:33
  362.8 14.3 %attback.1 = (bf16[128,1024]{1,0:T(8,128)(2,1)}, f32[512,1024]{1,0:T(8,128)}, bf16[512,1024]{1,0:T(8,128)(2,1)}) custom-call(bf16[128,1024]{1,0:T(8,128)(2,1)} %fusion.108.dh_ref, bf16[512,1152]{1,0:T(8,128)(2,1)} %constant_dynamic-update-slice_fusion.4.own_ref, bf16[512,1152]{1,0:T(8,128)(2,1)} %copy-done.17, bf16[1024,1024]{1,0:T(8,128)(2,1)} %copy-done, ...), custom_call_target="tpu_custom_call" | custom-call | tf_op jit(solution)/shard_map/attback/pallas_call | solution.py:729
  385.6 3.0 fusion.30
  399.5 3.0 fusion.133
  402.5 38.3 %collective-permute-done.90 = bf16[2,512,256]{2,1,0:T(8,128)(2,1)} collective-permute-done((bf16[2,512,256]{2,1,0:T(8,128)(2,1)}, bf16[2,512,256]{2,1,0:T(8,128)(2,1)}, u32[]{:S(2)}, u32[]{:S(2)}) %collective-permute-start.90) | collective-permute-done | bytes 524320 | tf_op jit(solution)/shard_map/ppermute | solution.py:33
  445.3 8.5 %collective-permute-done.55 = bf16[128,1024]{1,0:T(8,128)(2,1)S(1)} collective-permute-done((bf16[128,1024]{1,0:T(8,128)(2,1)S(1)}, bf16[128,1024]{1,0:T(8,128)(2,1)S(1)}, u32[]{:S(2)}, u32[]{:S(2)}) %collective-permute-start.55) | collective-permute-done | bytes 262176 | tf_op jit(solution)/shard_map/ppermute | solution.py:33
  456.0 3.1 backproj.1
  459.2 10.8 %collective-permute-done.86 = bf16[2,256,1024]{2,1,0:T(8,128)(2,1)S(1)} collective-permute-done((bf16[2,256,1024]{2,1,0:T(8,128)(2,1)S(1)}, bf16[2,256,1024]{2,1,0:T(8,128)(2,1)S(1)}, u32[]{:S(2)}, u32[]{:S(2)}) %collective-permute-start.86) | collective-permute-done | bytes 1048608 | tf_op jit(solution)/shard_map/ppermute | solution.py:33
  472.4 2.7 collective-permute-start.67
  481.5 3.1 collective-permute-start.83
  492.3 2.9 bitcast_select_fusion
  505.1 3.1 collective-permute-start.69
  509.6 3.1 collective-permute-start.62
  515.3 2.7 collective-permute-start.74
  518.8 4.4 collective-permute-done.72
  523.2 3.1 collective-permute-done.73
  527.0 2.7 collective-permute-start.76
  532.1 3.6 collective-permute-done.77
  (439 shorter events, 177.6 us)
Async XLA Ops:
  3.0 53.5 %collective-permute-start = (bf16[32,2176]{1,0:T(8,128)(2,1)}, bf16[32,2176]{1,0:T(8,128)(2,1)}, u32[]{:S(2)}, u32[]{:S(2)}) collective-permute-start(bf16[32,2176]{1,0:T(8,128)(2,1)} %concatenate.38), channel_id=1, source_target_pairs={{0,8},{8,0},{16,24},{24,16},{1,9},{9,1},{17,25},{25,17},{2,10},{10... | collective-permute-start | bytes 417800 | tf_op jit(solution)/shard_map/ppermute | solution.py:33
  6.1 50.5 %collective-permute-start.1 = (bf16[32,2176]{1,0:T(8,128)(2,1)}, bf16[32,2176]{1,0:T(8,128)(2,1)}, u32[]{:S(2)}, u32[]{:S(2)}) collective-permute-start(bf16[32,2176]{1,0:T(8,128)(2,1)} %concatenate.38), channel_id=1, source_target_pairs={{0,16},{8,24},{16,0},{24,8},{1,17},{9,25},{17,1},{25,9},{2,18},{10... | collective-permute-start | bytes 417800 | tf_op jit(solution)/shard_map/ppermute | solution.py:33
  8.7 49.5 %collective-permute-start.2 = (bf16[32,2176]{1,0:T(8,128)(2,1)}, bf16[32,2176]{1,0:T(8,128)(2,1)}, u32[]{:S(2)}, u32[]{:S(2)}) collective-permute-start(bf16[32,2176]{1,0:T(8,128)(2,1)} %concatenate.38), channel_id=1, source_target_pairs={{0,24},{8,16},{16,8},{24,0},{1,25},{9,17},{17,9},{25,1},{2,26},{10... | collective-permute-start | bytes 417800 | tf_op jit(solution)/shard_map/ppermute | solution.py:33
  11.0 24.8 %collective-permute-start.14 = (bf16[32,1152]{1,0:T(8,128)(2,1)}, bf16[32,1152]{1,0:T(8,128)(2,1)}, u32[]{:S(2)}, u32[]{:S(2)}) collective-permute-start(bf16[32,1152]{1,0:T(8,128)(2,1)} %concatenate.41), channel_id=1, source_target_pairs={{0,8},{8,0},{16,24},{24,16},{1,9},{9,1},{17,25},{25,17},{2,10},{10... | collective-permute-start | bytes 221192 | tf_op jit(solution)/shard_map/ppermute | solution.py:33
  11.9 25.4 %collective-permute-start.15 = (bf16[32,1152]{1,0:T(8,128)(2,1)}, bf16[32,1152]{1,0:T(8,128)(2,1)}, u32[]{:S(2)}, u32[]{:S(2)}) collective-permute-start(bf16[32,1152]{1,0:T(8,128)(2,1)} %concatenate.41), channel_id=1, source_target_pairs={{0,16},{8,24},{16,0},{24,8},{1,17},{9,25},{17,1},{25,9},{2,18},{10... | collective-permute-start | bytes 221192 | tf_op jit(solution)/shard_map/ppermute | solution.py:33
  37.3 63.6 %collective-permute-start.32 = (bf16[2,512,256]{2,1,0:T(8,128)(2,1)}, bf16[2,512,256]{2,1,0:T(8,128)(2,1)}, u32[]{:S(2)}, u32[]{:S(2)}) collective-permute-start(bf16[2,512,256]{2,1,0:T(8,128)(2,1)} %get-tuple-element.134), channel_id=1, source_target_pairs={{0,16},{8,24},{16,0},{24,8},{1,17},{9,25},{17,1},{25,9},{2,18},{10... | collective-permute-start | bytes 1572872 | tf_op jit(solution)/shard_map/ppermute | solution.py:33
  43.0 71.2 %collective-permute-start.34 = (bf16[2,512,256]{2,1,0:T(8,128)(2,1)}, bf16[2,512,256]{2,1,0:T(8,128)(2,1)}, u32[]{:S(2)}, u32[]{:S(2)}) collective-permute-start(bf16[2,512,256]{2,1,0:T(8,128)(2,1)} %get-tuple-element.133), channel_id=1, source_target_pairs={{0,8},{8,0},{16,24},{24,16},{1,9},{9,1},{17,25},{25,17},{2,10},{10... | collective-permute-start | bytes 1572872 | tf_op jit(solution)/shard_map/ppermute | solution.py:33
  56.6 24.7 %collective-permute-start.17 = (bf16[128,1152]{1,0:T(8,128)(2,1)}, bf16[128,1152]{1,0:T(8,128)(2,1)}, u32[]{:S(2)}, u32[]{:S(2)}) collective-permute-start(bf16[128,1152]{1,0:T(8,128)(2,1)} %pad_maximum_fusion.3), channel_id=1, source_target_pairs={{0,2},{1,3},{2,0},{3,1},{4,6},{5,7},{6,4},{7,5},{8,10},{9,11},{10,... | collective-permute-start | bytes 884744 | tf_op jit(solution)/shard_map/ppermute | solution.py:33
  58.1 25.4 %collective-permute-start.18 = (bf16[128,1152]{1,0:T(8,128)(2,1)}, bf16[128,1152]{1,0:T(8,128)(2,1)}, u32[]{:S(2)}, u32[]{:S(2)}) collective-permute-start(bf16[128,1152]{1,0:T(8,128)(2,1)} %pad_maximum_fusion.3), channel_id=1, source_target_pairs={{0,4},{1,5},{2,6},{3,7},{4,0},{5,1},{6,2},{7,3},{8,12},{9,13},{10,... | collective-permute-start | bytes 884744 | tf_op jit(solution)/shard_map/ppermute | solution.py:33
  83.5 27.8 %collective-permute-start.23 = (bf16[256,1152]{1,0:T(8,128)(2,1)}, bf16[256,1152]{1,0:T(8,128)(2,1)}, u32[]{:S(2)}, u32[]{:S(2)}) collective-permute-start(bf16[256,1152]{1,0:T(8,128)(2,1)} %pad_maximum_fusion.1.refs_14_), channel_id=1, source_target_pairs={{0,4},{1,5},{2,6},{3,7},{4,0},{5,1},{6,2},{7,3},{8,12},{9,13},{10,... | collective-permute-start | bytes 1769480 | tf_op jit(solution)/shard_map/ppermute | solution.py:33
  87.4 29.3 %collective-permute-start.24 = (bf16[256,1152]{1,0:T(8,128)(2,1)}, bf16[256,1152]{1,0:T(8,128)(2,1)}, u32[]{:S(2)}, u32[]{:S(2)}) collective-permute-start(bf16[256,1152]{1,0:T(8,128)(2,1)} %pad_maximum_fusion.1.refs_14_), channel_id=1, source_target_pairs={{0,6},{1,7},{2,4},{3,5},{4,2},{5,3},{6,0},{7,1},{8,14},{9,15},{10,... | collective-permute-start | bytes 1769480 | tf_op jit(solution)/shard_map/ppermute | solution.py:33
  100.0 35.5 %collective-permute-start.25 = (bf16[256,1152]{1,0:T(8,128)(2,1)}, bf16[256,1152]{1,0:T(8,128)(2,1)}, u32[]{:S(2)}, u32[]{:S(2)}) collective-permute-start(bf16[256,1152]{1,0:T(8,128)(2,1)} %pad_maximum_fusion.1.refs_14_), channel_id=1, source_target_pairs={{0,1},{1,0},{2,3},{3,2},{4,5},{5,4},{6,7},{7,6},{8,9},{9,8},{10,11... | collective-permute-start | bytes 1769480 | tf_op jit(solution)/shard_map/ppermute | solution.py:33
  100.9 23.7 %collective-permute-start.3 = (bf16[128,2176]{1,0:T(8,128)(2,1)S(1)}, bf16[128,2176]{1,0:T(8,128)(2,1)S(1)}, u32[]{:S(2)}, u32[]{:S(2)}) collective-permute-start(bf16[128,2176]{1,0:T(8,128)(2,1)S(1)} %pad_maximum_fusion.2.refs_5_.refs_0_), channel_id=1, source_target_pairs={{0,2},{1,3},{2,0},{3,1},{4,6},{5,7},{6,4},{7,5},{8,10},{9,11},{10,... | collective-permute-start | bytes 1671176 | tf_op jit(solution)/shard_map/ppermute | solution.py:33
  111.3 24.2 %collective-permute-start.4 = (bf16[128,2176]{1,0:T(8,128)(2,1)S(1)}, bf16[128,2176]{1,0:T(8,128)(2,1)}, u32[]{:S(2)}, u32[]{:S(2)}) collective-permute-start(bf16[128,2176]{1,0:T(8,128)(2,1)S(1)} %pad_maximum_fusion.2.refs_5_.refs_0_), channel_id=1, source_target_pairs={{0,4},{1,5},{2,6},{3,7},{4,0},{5,1},{6,2},{7,3},{8,12},{9,13},{10,... | collective-permute-start | bytes 1671176 | tf_op jit(solution)/shard_map/ppermute | solution.py:33
  114.2 22.8 %collective-permute-start.5 = (bf16[128,2176]{1,0:T(8,128)(2,1)S(1)}, bf16[128,2176]{1,0:T(8,128)(2,1)}, u32[]{:S(2)}, u32[]{:S(2)}) collective-permute-start(bf16[128,2176]{1,0:T(8,128)(2,1)S(1)} %pad_maximum_fusion.2.refs_5_.refs_0_), channel_id=1, source_target_pairs={{0,6},{1,7},{2,4},{3,5},{4,2},{5,3},{6,0},{7,1},{8,14},{9,15},{10,... | collective-permute-start | bytes 1671176 | tf_op jit(solution)/shard_map/ppermute | solution.py:33
  124.6 44.2 %collective-permute-start.29 = (bf16[2,256,1024]{2,1,0:T(8,128)(2,1)}, bf16[2,256,1024]{2,1,0:T(8,128)(2,1)}, u32[]{:S(2)}, u32[]{:S(2)}) collective-permute-start(bf16[2,256,1024]{2,1,0:T(8,128)(2,1)} %get-tuple-element.98), channel_id=1, source_target_pairs={{0,8},{8,0},{16,24},{24,16},{1,9},{9,1},{17,25},{25,17},{2,10},{10... | collective-permute-start | bytes 3145736 | tf_op jit(solution)/shard_map/ppermute | solution.py:33
  135.5 22.8 %collective-permute-start.33 = (bf16[2,512,256]{2,1,0:T(8,128)(2,1)}, bf16[2,512,256]{2,1,0:T(8,128)(2,1)}, u32[]{:S(2)}, u32[]{:S(2)}) collective-permute-start(bf16[2,512,256]{2,1,0:T(8,128)(2,1)} %collective-permute-done.32), channel_id=1, source_target_pairs={{0,8},{8,0},{16,24},{24,16},{1,9},{9,1},{17,25},{25,17},{2,10},{10... | collective-permute-start | bytes 1572872 | tf_op jit(solution)/shard_map/ppermute | solution.py:33
  135.5 24.1 %collective-permute-start.7 = (bf16[128,2176]{1,0:T(8,128)(2,1)S(1)}, bf16[128,2176]{1,0:T(8,128)(2,1)}, u32[]{:S(2)}, u32[]{:S(2)}) collective-permute-start(bf16[128,2176]{1,0:T(8,128)(2,1)S(1)} %collective-permute-done.3.refs_6_.refs_1_), channel_id=1, source_target_pairs={{0,1},{1,0},{2,3},{3,2},{4,5},{5,4},{6,7},{7,6},{8,9},{9,8},{10,11... | collective-permute-start | bytes 1671176 | tf_op jit(solution)/shard_map/ppermute | solution.py:33
  137.0 24.3 %collective-permute-start.8 = (bf16[128,2176]{1,0:T(8,128)(2,1)}, bf16[128,2176]{1,0:T(8,128)(2,1)}, u32[]{:S(2)}, u32[]{:S(2)}) collective-permute-start(bf16[128,2176]{1,0:T(8,128)(2,1)} %collective-permute-done.4.refs_7_.refs_2_), channel_id=1, source_target_pairs={{0,1},{1,0},{2,3},{3,2},{4,5},{5,4},{6,7},{7,6},{8,9},{9,8},{10,11... | collective-permute-start | bytes 1671176 | tf_op jit(solution)/shard_map/ppermute | solution.py:33
  138.3 23.6 %collective-permute-start.9 = (bf16[128,2176]{1,0:T(8,128)(2,1)}, bf16[128,2176]{1,0:T(8,128)(2,1)}, u32[]{:S(2)}, u32[]{:S(2)}) collective-permute-start(bf16[128,2176]{1,0:T(8,128)(2,1)} %collective-permute-done.5.refs_8_.refs_3_), channel_id=1, source_target_pairs={{0,1},{1,0},{2,3},{3,2},{4,5},{5,4},{6,7},{7,6},{8,9},{9,8},{10,11... | collective-permute-start | bytes 1671176 | tf_op jit(solution)/shard_map/ppermute | solution.py:33
  158.3 45.1 %collective-permute-start.30 = (bf16[2,256,1024]{2,1,0:T(8,128)(2,1)}, bf16[2,256,1024]{2,1,0:T(8,128)(2,1)}, u32[]{:S(2)}, u32[]{:S(2)}) collective-permute-start(bf16[2,256,1024]{2,1,0:T(8,128)(2,1)} %dynamic-slice_bitcast_fusion), channel_id=1, source_target_pairs={{0,16},{8,24},{16,0},{24,8},{1,17},{9,25},{17,1},{25,9},{2,18},{10... | collective-permute-start | bytes 3145736 | tf_op jit(solution)/shard_map/ppermute | solution.py:33
  159.6 47.5 %collective-permute-start.20 = (bf16[512,1152]{1,0:T(8,128)(2,1)}, bf16[512,1152]{1,0:T(8,128)(2,1)S(1)}, u32[]{:S(2)}, u32[]{:S(2)}) collective-permute-start(bf16[512,1152]{1,0:T(8,128)(2,1)} %constant_dynamic-update-slice_fusion.4.own_ref), channel_id=1, source_target_pairs={{0,1},{1,0},{2,3},{3,2},{4,5},{5,4},{6,7},{7,6},{8,9},{9,8},{10,11... | collective-permute-start | bytes 3538952 | tf_op jit(solution)/shard_map/ppermute | solution.py:33
  161.3 44.4 %collective-permute-start.26 = (bf16[256,1152]{1,0:T(8,128)(2,1)S(1)}, bf16[256,1152]{1,0:T(8,128)(2,1)S(1)}, u32[]{:S(2)}, u32[]{:S(2)}) collective-permute-start(bf16[256,1152]{1,0:T(8,128)(2,1)S(1)} %copy-done.39), channel_id=1, source_target_pairs={{0,1},{1,0},{2,3},{3,2},{4,5},{5,4},{6,7},{7,6},{8,9},{9,8},{10,11... | collective-permute-start | bytes 1769480 | tf_op jit(solution)/shard_map/ppermute | solution.py:33
  182.5 43.4 %collective-permute-start.27 = (bf16[256,1152]{1,0:T(8,128)(2,1)}, bf16[256,1152]{1,0:T(8,128)(2,1)S(1)}, u32[]{:S(2)}, u32[]{:S(2)}) collective-permute-start(bf16[256,1152]{1,0:T(8,128)(2,1)} %collective-permute-done.23.refs_16_), channel_id=1, source_target_pairs={{0,1},{1,0},{2,3},{3,2},{4,5},{5,4},{6,7},{7,6},{8,9},{9,8},{10,11... | collective-permute-start | bytes 1769480 | tf_op jit(solution)/shard_map/ppermute | solution.py:33
  182.5 56.5 %collective-permute-start.28 = (bf16[256,1152]{1,0:T(8,128)(2,1)}, bf16[256,1152]{1,0:T(8,128)(2,1)}, u32[]{:S(2)}, u32[]{:S(2)}) collective-permute-start(bf16[256,1152]{1,0:T(8,128)(2,1)} %collective-permute-done.24.refs_17_), channel_id=1, source_target_pairs={{0,1},{1,0},{2,3},{3,2},{4,5},{5,4},{6,7},{7,6},{8,9},{9,8},{10,11... | collective-permute-start | bytes 1769480 | tf_op jit(solution)/shard_map/ppermute | solution.py:33
  205.7 60.1 %collective-permute-start.31 = (bf16[2,256,1024]{2,1,0:T(8,128)(2,1)}, bf16[2,256,1024]{2,1,0:T(8,128)(2,1)S(1)}, u32[]{:S(2)}, u32[]{:S(2)}) collective-permute-start(bf16[2,256,1024]{2,1,0:T(8,128)(2,1)} %collective-permute-done.30), channel_id=1, source_target_pairs={{0,8},{8,0},{16,24},{24,16},{1,9},{9,1},{17,25},{25,17},{2,10},{10... | collective-permute-start | bytes 3145736 | tf_op jit(solution)/shard_map/ppermute | solution.py:33
  237.1 24.5 %collective-permute-start.37 = (bf16[256,1024]{1,0:T(8,128)(2,1)S(1)}, bf16[256,1024]{1,0:T(8,128)(2,1)}, u32[]{:S(2)}, u32[]{:S(2)}) collective-permute-start(bf16[256,1024]{1,0:T(8,128)(2,1)S(1)} %constant_dynamic-update-slice_fusion.19.refs_6_), channel_id=1, source_target_pairs={{0,4},{1,5},{2,6},{3,7},{4,0},{5,1},{6,2},{7,3},{8,12},{9,13},{10,... | collective-permute-start | bytes 1572872 | tf_op jit(solution)/shard_map/ppermute | solution.py:33
  237.6 24.0 %collective-permute-start.38 = (bf16[256,1024]{1,0:T(8,128)(2,1)S(1)}, bf16[256,1024]{1,0:T(8,128)(2,1)}, u32[]{:S(2)}, u32[]{:S(2)}) collective-permute-start(bf16[256,1024]{1,0:T(8,128)(2,1)S(1)} %constant_dynamic-update-slice_fusion.19.refs_6_), channel_id=1, source_target_pairs={{0,6},{1,7},{2,4},{3,5},{4,2},{5,3},{6,0},{7,1},{8,14},{9,15},{10,... | collective-permute-start | bytes 1572872 | tf_op jit(solution)/shard_map/ppermute | solution.py:33
  245.1 21.7 %collective-permute-start.39 = (bf16[256,1024]{1,0:T(8,128)(2,1)S(1)}, bf16[256,1024]{1,0:T(8,128)(2,1)S(1)}, u32[]{:S(2)}, u32[]{:S(2)}) collective-permute-start(bf16[256,1024]{1,0:T(8,128)(2,1)S(1)} %constant_dynamic-update-slice_fusion.19.refs_6_), channel_id=1, source_target_pairs={{0,1},{1,0},{2,3},{3,2},{4,5},{5,4},{6,7},{7,6},{8,9},{9,8},{10,11... | collective-permute-start | bytes 1572872 | tf_op jit(solution)/shard_map/ppermute | solution.py:33
  310.4 31.6 %collective-permute-start.85 = (bf16[2,256,1024]{2,1,0:T(8,128)(2,1)S(1)}, bf16[2,256,1024]{2,1,0:T(8,128)(2,1)S(1)}, u32[]{:S(2)}, u32[]{:S(2)}) collective-permute-start(bf16[2,256,1024]{2,1,0:T(8,128)(2,1)S(1)} %get-tuple-element.104), channel_id=1, source_target_pairs={{0,8},{8,0},{16,24},{24,16},{1,9},{9,1},{17,25},{25,17},{2,10},{10... | collective-permute-start | bytes 3145736 | tf_op jit(solution)/shard_map/ppermute | solution.py:33
  310.5 36.3 %collective-permute-start.43 = (bf16[1024,1024]{1,0:T(8,128)(2,1)S(1)}, bf16[1024,1024]{1,0:T(8,128)(2,1)S(1)}, u32[]{:S(2)}, u32[]{:S(2)}) collective-permute-start(bf16[1024,1024]{1,0:T(8,128)(2,1)S(1)} %copy-done.66), channel_id=1, source_target_pairs={{0,1},{1,0},{2,3},{3,2},{4,5},{5,4},{6,7},{7,6},{8,9},{9,8},{10,11... | collective-permute-start | bytes 6291464 | tf_op jit(solution)/shard_map/ppermute | solution.py:33
  313.1 31.6 %collective-permute-start.46 = (bf16[256,1152]{1,0:T(8,128)(2,1)S(1)}, bf16[256,1152]{1,0:T(8,128)(2,1)S(1)}, u32[]{:S(2)}, u32[]{:S(2)}) collective-permute-start(bf16[256,1152]{1,0:T(8,128)(2,1)S(1)} %get-tuple-element.108), channel_id=1, source_target_pairs={{0,2},{1,3},{2,0},{3,1},{4,6},{5,7},{6,4},{7,5},{8,10},{9,11},{10,... | collective-permute-start | bytes 1769480 | tf_op jit(solution)/shard_map/ppermute | solution.py:33
  313.7 31.0 %collective-permute-start.47 = (bf16[256,1152]{1,0:T(8,128)(2,1)S(1)}, bf16[256,1152]{1,0:T(8,128)(2,1)S(1)}, u32[]{:S(2)}, u32[]{:S(2)}) collective-permute-start(bf16[256,1152]{1,0:T(8,128)(2,1)S(1)} %get-tuple-element.110), channel_id=1, source_target_pairs={{0,4},{1,5},{2,6},{3,7},{4,0},{5,1},{6,2},{7,3},{8,12},{9,13},{10,... | collective-permute-start | bytes 1769480 | tf_op jit(solution)/shard_map/ppermute | solution.py:33
  319.8 24.9 %collective-permute-start.48 = (bf16[256,1152]{1,0:T(8,128)(2,1)S(1)}, bf16[256,1152]{1,0:T(8,128)(2,1)S(1)}, u32[]{:S(2)}, u32[]{:S(2)}) collective-permute-start(bf16[256,1152]{1,0:T(8,128)(2,1)S(1)} %get-tuple-element.109), channel_id=1, source_target_pairs={{0,6},{1,7},{2,4},{3,5},{4,2},{5,3},{6,0},{7,1},{8,14},{9,15},{10,... | collective-permute-start | bytes 1769480 | tf_op jit(solution)/shard_map/ppermute | solution.py:33
  350.0 31.5 %collective-permute-start.44 = (bf16[256,1024]{1,0:T(8,128)(2,1)S(1)}, bf16[256,1024]{1,0:T(8,128)(2,1)}, u32[]{:S(2)}, u32[]{:S(2)}) collective-permute-start(bf16[256,1024]{1,0:T(8,128)(2,1)S(1)} %get-tuple-element.114), channel_id=1, source_target_pairs={{0,2},{1,3},{2,0},{3,1},{4,6},{5,7},{6,4},{7,5},{8,10},{9,11},{10,... | collective-permute-start | bytes 1572872 | tf_op jit(solution)/shard_map/ppermute | solution.py:33
  350.6 31.0 %collective-permute-start.50 = (bf16[256,1024]{1,0:T(8,128)(2,1)S(1)}, bf16[256,1024]{1,0:T(8,128)(2,1)}, u32[]{:S(2)}, u32[]{:S(2)}) collective-permute-start(bf16[256,1024]{1,0:T(8,128)(2,1)S(1)} %get-tuple-element.116), channel_id=1, source_target_pairs={{0,4},{1,5},{2,6},{3,7},{4,0},{5,1},{6,2},{7,3},{8,12},{9,13},{10,... | collective-permute-start | bytes 1572872 | tf_op jit(solution)/shard_map/ppermute | solution.py:33
  351.3 32.3 %collective-permute-start.51 = (bf16[256,1024]{1,0:T(8,128)(2,1)S(1)}, bf16[256,1024]{1,0:T(8,128)(2,1)}, u32[]{:S(2)}, u32[]{:S(2)}) collective-permute-start(bf16[256,1024]{1,0:T(8,128)(2,1)S(1)} %get-tuple-element.115), channel_id=1, source_target_pairs={{0,6},{1,7},{2,4},{3,5},{4,2},{5,3},{6,0},{7,1},{8,14},{9,15},{10,... | collective-permute-start | bytes 1572872 | tf_op jit(solution)/shard_map/ppermute | solution.py:33
  381.5 77.5 %collective-permute-start.89 = (bf16[2,256,1024]{2,1,0:T(8,128)(2,1)}, bf16[2,256,1024]{2,1,0:T(8,128)(2,1)}, u32[]{:S(2)}, u32[]{:S(2)}) collective-permute-start(bf16[2,256,1024]{2,1,0:T(8,128)(2,1)} %get-tuple-element.103), channel_id=1, source_target_pairs={{0,8},{8,0},{16,24},{24,16},{1,9},{9,1},{17,25},{25,17},{2,10},{10... | collective-permute-start | bytes 3145736 | tf_op jit(solution)/shard_map/ppermute | solution.py:33
  381.6 59.2 %collective-permute-start.90 = (bf16[2,512,256]{2,1,0:T(8,128)(2,1)}, bf16[2,512,256]{2,1,0:T(8,128)(2,1)}, u32[]{:S(2)}, u32[]{:S(2)}) collective-permute-start(bf16[2,512,256]{2,1,0:T(8,128)(2,1)} %get-tuple-element.111), channel_id=1, source_target_pairs={{0,8},{8,0},{16,24},{24,16},{1,9},{9,1},{17,25},{25,17},{2,10},{10... | collective-permute-start | bytes 1572872 | tf_op jit(solution)/shard_map/ppermute | solution.py:33
  392.2 49.1 %collective-permute-start.88 = (bf16[2,512,256]{2,1,0:T(8,128)(2,1)}, bf16[2,512,256]{2,1,0:T(8,128)(2,1)S(1)}, u32[]{:S(2)}, u32[]{:S(2)}) collective-permute-start(bf16[2,512,256]{2,1,0:T(8,128)(2,1)} %add_convert_fusion.1), channel_id=1, source_target_pairs={{0,16},{8,24},{16,0},{24,8},{1,17},{9,25},{17,1},{25,9},{2,18},{10... | collective-permute-start | bytes 1572872 | tf_op jit(solution)/shard_map/ppermute | solution.py:33
  395.2 74.8 %collective-permute-start.86 = (bf16[2,256,1024]{2,1,0:T(8,128)(2,1)S(1)}, bf16[2,256,1024]{2,1,0:T(8,128)(2,1)S(1)}, u32[]{:S(2)}, u32[]{:S(2)}) collective-permute-start(bf16[2,256,1024]{2,1,0:T(8,128)(2,1)S(1)} %copy-done.32), channel_id=1, source_target_pairs={{0,16},{8,24},{16,0},{24,8},{1,17},{9,25},{17,1},{25,9},{2,18},{10... | collective-permute-start | bytes 3145736 | tf_op jit(solution)/shard_map/ppermute | solution.py:33
  398.9 44.9 %collective-permute-start.54 = (bf16[128,1024]{1,0:T(8,128)(2,1)S(1)}, bf16[128,1024]{1,0:T(8,128)(2,1)S(1)}, u32[]{:S(2)}, u32[]{:S(2)}) collective-permute-start(bf16[128,1024]{1,0:T(8,128)(2,1)S(1)} %get-tuple-element.130), channel_id=1, source_target_pairs={{0,2},{1,3},{2,0},{3,1},{4,6},{5,7},{6,4},{7,5},{8,10},{9,11},{10,... | collective-permute-start | bytes 786440 | tf_op jit(solution)/shard_map/ppermute | solution.py:33
  443.8 28.3 %collective-permute-start.79 = (bf16[128,1024]{1,0:T(8,128)(2,1)S(1)}, bf16[128,1024]{1,0:T(8,128)(2,1)S(1)}, u32[]{:S(2)}, u32[]{:S(2)}) collective-permute-start(bf16[128,1024]{1,0:T(8,128)(2,1)S(1)} %get-tuple-element.121), channel_id=1, source_target_pairs={{0,2},{1,3},{2,0},{3,1},{4,6},{5,7},{6,4},{7,5},{8,10},{9,11},{10,... | collective-permute-start | bytes 786440 | tf_op jit(solution)/shard_map/ppermute | solution.py:33
  459.1 22.4 %collective-permute-start.52 = (bf16[128,1024]{1,0:T(8,128)(2,1)}, bf16[128,1024]{1,0:T(8,128)(2,1)}, u32[]{:S(2)}, u32[]{:S(2)}) collective-permute-start(bf16[128,1024]{1,0:T(8,128)(2,1)} %slice.516), channel_id=1, source_target_pairs={{0,16},{8,24},{16,0},{24,8},{1,17},{9,25},{17,1},{25,9},{2,18},{10... | collective-permute-start | bytes 786440 | tf_op jit(solution)/shard_map/ppermute | solution.py:33
  470.0 25.6 %collective-permute-start.65 = (bf16[128,1024]{1,0:T(8,128)(2,1)}, bf16[128,1024]{1,0:T(8,128)(2,1)}, u32[]{:S(2)}, u32[]{:S(2)}) collective-permute-start(bf16[128,1024]{1,0:T(8,128)(2,1)} %get-tuple-element.127), channel_id=1, source_target_pairs={{0,2},{1,3},{2,0},{3,1},{4,6},{5,7},{6,4},{7,5},{8,10},{9,11},{10,... | collective-permute-start | bytes 786440 | tf_op jit(solution)/shard_map/ppermute | solution.py:33
  472.1 24.9 %collective-permute-start.66 = (bf16[128,1024]{1,0:T(8,128)(2,1)}, bf16[128,1024]{1,0:T(8,128)(2,1)}, u32[]{:S(2)}, u32[]{:S(2)}) collective-permute-start(bf16[128,1024]{1,0:T(8,128)(2,1)} %get-tuple-element.129), channel_id=1, source_target_pairs={{0,4},{1,5},{2,6},{3,7},{4,0},{5,1},{6,2},{7,3},{8,12},{9,13},{10,... | collective-permute-start | bytes 786440 | tf_op jit(solution)/shard_map/ppermute | solution.py:33
  472.4 24.6 %collective-permute-start.67 = (bf16[128,1024]{1,0:T(8,128)(2,1)}, bf16[128,1024]{1,0:T(8,128)(2,1)}, u32[]{:S(2)}, u32[]{:S(2)}) collective-permute-start(bf16[128,1024]{1,0:T(8,128)(2,1)} %get-tuple-element.128), channel_id=1, source_target_pairs={{0,6},{1,7},{2,4},{3,5},{4,2},{5,3},{6,0},{7,1},{8,14},{9,15},{10,... | collective-permute-start | bytes 786440 | tf_op jit(solution)/shard_map/ppermute | solution.py:33
  476.8 23.1 %collective-permute-start.82 = (bf16[32,1024]{1,0:T(8,128)(2,1)}, bf16[32,1024]{1,0:T(8,128)(2,1)S(1)}, u32[]{:S(2)}, u32[]{:S(2)}) collective-permute-start(bf16[32,1024]{1,0:T(8,128)(2,1)} %get-tuple-element.135), channel_id=1, source_target_pairs={{0,8},{8,0},{16,24},{24,16},{1,9},{9,1},{17,25},{25,17},{2,10},{10... | collective-permute-start | bytes 196616 | tf_op jit(solution)/shard_map/ppermute | solution.py:33
  (111 other events, 1491.2 us)
